TPU v7x, 32 devices: a whole 2x2x4 slice. The times are simulated.
32 devices in a mesh: pair: 2 (over x), code: 2 (over core), dp: 8 (over z, y).
Axes of the slice: x: 2, y: 2, z: 4, core: 2. Of those that a mesh axis runs over, the one named last changes fastest.
Arguments:
- samples: bfloat16 [1536, 1024], P('dp'), may hold values from -48 to 48
- codebooks: bfloat16 [2, 16384, 1024], P('pair', 'code'), may hold values from -0.15625 to 0.15625
Outputs:
- new_codebooks: float32 [2, 16384, 1024], P('pair', ('code', 'dp'))
All inputs are finite; a program needn't handle non-finite values.
Results may differ from a plain program's by a relative error of at most 0.015.
Values may be sent and summed in bfloat16 or wider, within the bound.
No kernel may reach another device: no remote copies, remote signals or barrier semaphores. Data moves between devices by JAX's collectives and lax.ppermute only.
A program may use at most 192 MiB of HBM per device.

v0:
```python
import jax
import jax.numpy as jnp
from jax import lax
from jax.sharding import PartitionSpec as P

smoothing = 0.5


def joined(value, axis, join):
    gathered = jax.tree.map(
        lambda a, kind: lax.all_gather(a.astype(kind), axis),
        value,
        (jnp.bfloat16, jnp.bfloat16, jnp.bfloat16),
    )

    def take(source):
        return jax.tree.map(
            lambda a, own: lax.dynamic_index_in_dim(a, source, 0, False).astype(own.dtype),
            gathered,
            value,
        )

    return lax.fori_loop(
        1, lax.axis_size(axis), lambda source, state: join(state, take(source)), take(0)
    )


def from_partner(value, axis, distance):
    return lax.ppermute(value, axis, [(i, i ^ 1 << distance) for i in range(lax.axis_size(axis))])


def scores_of(block, words, sq_norms):
    product = lax.dot_general(
        block, words, (((1,), (1,)), ((), ())), preferred_element_type=jnp.float32
    )
    return 2.0 * product - sq_norms[None, :]


def join_parts(earlier, later):
    top_a, total_a, summed_a = earlier
    top_b, total_b, summed_b = later
    top_val = jnp.maximum(top_a, top_b)
    scale_a = jnp.exp(top_a - top_val)
    scale_b = jnp.exp(top_b - top_val)
    return (top_val, total_a * scale_a + total_b * scale_b, summed_a * scale_a + summed_b * scale_b)


def shards(samples, codebooks):
    words = codebooks[0]
    words32 = words.astype(jnp.float32)
    sq_norms = jnp.sum(words32 * words32, axis=-1)
    logits = scores_of(samples, words, sq_norms)
    local_top = jnp.max(logits, axis=1, keepdims=True)
    expd = jnp.exp(logits - local_top)
    local_total = jnp.sum(expd, axis=1, keepdims=True)
    summed = jnp.dot(expd.astype(jnp.bfloat16), words, preferred_element_type=jnp.float32)
    top_val, total, summed = joined((local_top, local_total, summed), "code", join_parts)
    rebuilt = (summed / total).astype(jnp.bfloat16)
    partner = from_partner(rebuilt, "pair", 0)
    residual = (samples.astype(jnp.float32) - partner.astype(jnp.float32)).astype(jnp.bfloat16)
    second = scores_of(residual, words, sq_norms)
    second_top = jnp.max(second, axis=1, keepdims=True)
    global_top = lax.pmax(second_top, "code")
    second_exp = jnp.exp(second - global_top)
    global_total = lax.psum(jnp.sum(second_exp, axis=1, keepdims=True), "code")
    assign = (second_exp / global_total).astype(jnp.bfloat16)
    owners = lax.axis_size("dp")
    own_count = words.shape[0] // owners
    own_words = lax.dynamic_slice_in_dim(words32, lax.axis_index("dp") * own_count, own_count, 0)
    partial_value = lax.dot_general(
        assign, residual, (((0,), (0,)), ((), ())), preferred_element_type=jnp.float32
    )
    counts = jnp.sum(assign.astype(jnp.float32), axis=0)
    sums, counts = (
        lax.psum_scatter(partial_value, "dp", scatter_dimension=0, tiled=True),
        lax.psum_scatter(counts, "dp", scatter_dimension=0, tiled=True),
    )
    updated = (sums + smoothing * own_words) / (counts[:, None] + smoothing)
    return updated[None]


def solution(mesh):
    in_specs = (P("dp", None), P("pair", "code", None))
    out_specs = P("pair", ("code", "dp"), None)
    return jax.shard_map(shards, mesh=mesh, in_specs=in_specs, out_specs=out_specs, check_vma=False)
```

profile of v0, /device:TPU:0, one launch (start us, length us, event | category | flops | bytes accessed | tf_op | source)
XLA Modules:
  0.0 655.1 jit_solution(4621249740470149227)
XLA Ops:
  6.5 0.0 reduce-scatter.2.cloned.1.call-start
  6.5 0.0 copy-start.1
  6.5 7.2 %multiply_reduce_fusion = f32[8192]{0:T(1024)S(1)} fusion(bf16[1,8192,1024]{2,1,0:T(8,128)(2,1)} %param.3), kind=kLoop, calls=%fused_computation | loop fusion | flops 25157632 | bytes 16809984 | tf_op jit(solution)/shard_map/reduce_sum | solution.py:51
  13.8 0.0 copy-done.1
  13.8 14.1 %fusion.35 = (f32[192]{0:T(256)S(1)}, f32[192,8192]{1,0:T(8,128)}) fusion(f32[8192]{0:T(1024)S(1)} %multiply_reduce_fusion, bf16[192,1024]{1,0:T(8,128)(2,1)S(1)} %copy-done.1, bf16[1,8192,1024]{2,1,0:T(8,128)(2,1)} %param.3), kind=kOutput, calls=%fused_computation.37 | convolution fusion | flops 3225943808 | bytes 23495424 | tf_op jit(solution)/shard_map/dot_general | solution.py:33
  27.9 0.0 copy-start
  27.9 3.9 fusion.18
  31.8 0.7 copy-done
  32.5 9.2 %fusion.23 = bf16[192,1024]{1,0:T(8,128)(2,1)S(1)} fusion(bf16[1,8192,1024]{2,1,0:T(8,128)(2,1)} %param.3, f32[192,8192]{1,0:T(8,128)S(1)} %copy-done, f32[192]{0:T(256)S(1)} %get-tuple-element.36), kind=kOutput, calls=%fused_computation.21 | convolution fusion | flops 3224567808 | bytes 23462656 | tf_op jit(solution)/shard_map/dot_general | solution.py:56
  41.7 2.5 all-gather
  44.2 0.0 copy-done.3
  44.2 0.6 dynamic-slice
  45.5 0.2 dynamic-update-slice
  45.7 0.2 dynamic-update-slice.1
  46.0 2.7 all-reduce.3
  48.6 0.1 fusion.32
  48.7 0.2 fusion.30
  48.9 2.9 collective-permute-start
  51.8 9.4 %collective-permute-done = bf16[192,1024]{1,0:T(8,128)(2,1)S(1)} collective-permute-done((bf16[192,1024]{1,0:T(8,128)(2,1)S(1)}, bf16[192,1024]{1,0:T(8,128)(2,1)S(1)}, u32[]{:S(2)}, u32[]{:S(2)}) %collective-permute-start) | collective-permute-done | bytes 393248 | tf_op jit(solution)/shard_map/ppermute | solution.py:29
  61.3 14.1 %fusion.36 = (f32[192]{0:T(256)S(1)}, f32[192,8192]{1,0:T(8,128)}) fusion(f32[8192]{0:T(1024)S(1)} %multiply_reduce_fusion, bf16[1,8192,1024]{2,1,0:T(8,128)(2,1)} %param.3, bf16[192,1024]{1,0:T(8,128)(2,1)S(1)} %collective-permute-done, bf16[192,1024]{1,0:T(8,128)(2,1)S(1)} %copy-done.1), kind=kOutput, calls=%fused_computation.38 | convolution fusion | flops 3226730240 | bytes 23888640 | tf_op jit(solution)/shard_map/dot_general | solution.py:33
  75.4 2.4 pmax.7
  77.8 3.8 fusion.20
  81.6 2.5 psum.7
  84.1 3.6 convert_reduce_fusion
  87.6 13.1 %fusion.31 = f32[8192,1024]{1,0:T(8,128)} fusion(bf16[192,8192]{1,0:T(8,128)(2,1)S(1)} %get-tuple-element.22, bf16[192,1024]{1,0:T(8,128)(2,1)S(1)} %collective-permute-done, bf16[192,1024]{1,0:T(8,128)(2,1)S(1)} %copy-done.1), kind=kOutput, calls=%fused_computation.28 | convolution fusion | flops 3222011904 | bytes 37486592 | tf_op jit(solution)/shard_map/dot_general | solution.py:70
  100.7 0.0 reduce-scatter.2.cloned.1.call-update
  100.8 0.6 copy-done.2
  101.4 0.6 dynamic-slice.2
  102.6 18.7 %bitcast_convert_fusion = f32[8192,1024]{1,0:T(8,128)} fusion(bf16[1,8192,1024]{2,1,0:T(8,128)(2,1)} %param.3), kind=kLoop, calls=%fused_computation.5 | loop fusion | flops 8388608 | bytes 50331648 | tf_op jit(solution)/shard_map/convert_element_type | solution.py:50
  121.3 39.9 %all-reduce.2 = f32[8192]{0:T(1024)S(1)} all-reduce(f32[8192]{0:T(1024)S(1)} %get-tuple-element.21), channel_id=6, replica_groups=mesh['pair'=2,'code'=2,'dp'=8] {'dp'}, use_global_device_ids=true, to_apply=%region_9.10.clone | all-reduce | flops 8192 | bytes 65536
  161.2 480.2 %reduce-scatter.2.cloned.1.call-done = f32[1024,1024]{1,0:T(8,128)} async-done(((f32[8192,1024]{1,0:T(8,128)}), f32[1024,1024]{1,0:T(8,128)}) %reduce-scatter.2.cloned.1.call-update) | async-done | bytes 4194320 | tf_op jit(solution)/shard_map/reduce_scatter | solution.py:75
  641.4 6.8 %divide_bitcast_fusion = f32[1,1024,1024]{2,1,0:T(8,128)} fusion(f32[1024,1024]{1,0:T(8,128)} %reduce-scatter.2.cloned.1.call-done, f32[8192,1024]{1,0:T(8,128)} %bitcast_convert_fusion, s32[]{:T(128)S(6)} %select_n.12, f32[1024]{0:T(1024)S(1)} %dynamic-slice_add_fusion), kind=kLoop, calls=%fused_computation.19 | loop fusion | flops 3145728 | bytes 12587012 | tf_op jit(solution)/shard_map/broadcast_in_dim | solution.py:79
  (6 shorter events, 0.0 us)
Async XLA Ops:
  6.5 634.9 %reduce-scatter.2.cloned.1.call-start = ((), (), s32[]{:S(2)}) async-start(), calls=%async_computation.1 | async-start | bytes 37748736 | tf_op jit(solution)/shard_map/reduce_scatter | solution.py:75
  6.5 7.2 %copy-start.1 = (bf16[192,1024]{1,0:T(8,128)(2,1)S(1)}, bf16[192,1024]{1,0:T(8,128)(2,1)}, u32[]{:S(2)}) copy-start(bf16[192,1024]{1,0:T(8,128)(2,1)} %param.2) | copy-start | bytes 1179652
  27.9 4.6 copy-start
  32.5 11.8 %copy-start.3 = (u32[32]{0:T(128)S(1)}, u32[32]{0:T(128)}, u32[]{:S(2)}) copy-start(u32[32]{0:T(128)} %constant.46) | copy-start | bytes 388
  48.9 12.3 %collective-permute-start = (bf16[192,1024]{1,0:T(8,128)(2,1)S(1)}, bf16[192,1024]{1,0:T(8,128)(2,1)S(1)}, u32[]{:S(2)}, u32[]{:S(2)}) collective-permute-start(bf16[192,1024]{1,0:T(8,128)(2,1)S(1)} %fusion.30), channel_id=1, source_target_pairs={{0,16},{16,0},{1,17},{17,1},{2,18},{18,2},{3,19},{19,3},{4,20},{20... | collective-permute-start | bytes 1179656 | tf_op jit(solution)/shard_map/ppermute | solution.py:29
  100.7 0.7 copy-start.2
Sparse Core Ops, SparseCore 0:
  100.9 540.4 reduce-scatter.1
where the time goes:
time: 656 us; the launch traced here: 655 us
  waiting for transfers between devices  490 us (75%)
  matrix products  50.6 us (8%)
  blocking collectives  50 us (8%)
  other arithmetic  44.3 us (7%)
  between operations  14.8 us (2%)
    reduce_scatter x1, waiting for transfers between devices, shards(): lax.psum_scatter(partial_value, 'dp', scatter_dimension=0, tiled=True)  480 us
    unnamed x2, blocking collectives  42.6 us
    dot_general x2, matrix products, scores_of(): lax.dot_general(block, words, (((1,), (1,)), ((), ())), preferred_element...  28.2 us
    convert_element_type x1, other arithmetic, shards(): words32 = words.astype(jnp.float32)  18.7 us
    dot_general x1, matrix products, shards(): lax.dot_general(assign, residual, (((0,), (0,)), ((), ())), preferred_ele...  13.1 us
  transfers between devices with their start and end apart: 2, of which 2 were waited for; matrix products, arithmetic and copies ran while one was open for 3% of the time, Pallas kernels for 0%

commit v1 on v0

v1 whole, which is shorter than its diff:
```python
import functools

import jax
import jax.numpy as jnp
from jax import lax
from jax.experimental import pallas as pl
from jax.experimental.pallas import tpu as pltpu
from jax.sharding import PartitionSpec as P

smoothing = 0.5
f32, bf16 = jnp.float32, jnp.bfloat16
NT = (((1,), (1,)), ((), ()))
NN = (((1,), (0,)), ((), ()))
LANES = 128


def row_norms(words):
    wide = words.astype(f32)
    return jnp.sum(wide * wide, axis=1)


def first_kernel(core, s_ref, w_ref, mine, other, sq_ref, acc, top, total, twice):
    step = pl.program_id(0)
    rows, depth = s_ref.shape

    @pl.when(step == 0)
    def _():
        acc[...] = jnp.zeros_like(acc)
        top[...] = jnp.full_like(top, -jnp.inf)
        total[...] = jnp.zeros_like(total)
        twice[...] = s_ref[...] * 2

    words = w_ref[...]
    sq = row_norms(words)[None, :]
    sq_ref[...] = sq
    logits = lax.dot_general(twice[...], words, NT, preferred_element_type=f32) - sq
    old = top[...]
    new = jnp.maximum(old, jnp.max(logits, axis=1, keepdims=True))
    expd = jnp.exp(logits - new)
    scale = jnp.exp(old - new)
    top[...] = new
    total[...] = total[...] * scale + jnp.sum(expd, axis=1, keepdims=True)
    part = lax.dot_general(expd.astype(bf16), words, NN, preferred_element_type=f32)
    acc[...] = acc[...] * scale + part

    @pl.when(step == pl.num_programs(0) - 1)
    def _():
        half = rows // 2

        def put(ref, lo):
            at = slice(lo, lo + half)
            ref[:, :depth] = acc[at]
            ref[:, depth : depth + LANES] = jnp.broadcast_to(top[at], (half, LANES))
            ref[:, depth + LANES :] = jnp.broadcast_to(total[at], (half, LANES))

        @pl.when(core[0] == 0)
        def _():
            put(mine, 0)
            put(other, half)

        @pl.when(core[0] == 1)
        def _():
            put(mine, half)
            put(other, 0)


def first_pass(core, samples, words, tile):
    rows, depth = samples.shape
    count = words.shape[0]
    half = jax.ShapeDtypeStruct((rows // 2, depth + 2 * LANES), f32)
    return pl.pallas_call(
        first_kernel,
        grid=(count // tile,),
        in_specs=[
            pl.BlockSpec(memory_space=pltpu.SMEM),
            pl.BlockSpec((rows, depth), lambda t: (0, 0)),
            pl.BlockSpec((tile, depth), lambda t: (t, 0)),
        ],
        out_specs=[pl.BlockSpec(half.shape, lambda t: (0, 0))] * 2
        + [pl.BlockSpec((1, tile), lambda t: (0, t))],
        out_shape=[half, half, jax.ShapeDtypeStruct((1, count), f32)],
        scratch_shapes=[
            pltpu.VMEM((rows, depth), f32),
            pltpu.VMEM((rows, 1), f32),
            pltpu.VMEM((rows, 1), f32),
            pltpu.VMEM((rows, depth), bf16),
        ],
        name="first_pass",
        compiler_params=pltpu.CompilerParams(vmem_limit_bytes=24 * 2**20),
    )(core, samples, words)


def stats_kernel(a_ref, b_ref, w_ref, sq_ref, lse, top, total, twice):
    step = pl.program_id(0)
    half = a_ref.shape[0]

    @pl.when(step == 0)
    def _():
        top[...] = jnp.full_like(top, -jnp.inf)
        total[...] = jnp.zeros_like(total)
        twice[:half] = a_ref[...] * 2
        twice[half:] = b_ref[...] * 2

    logits = lax.dot_general(twice[...], w_ref[...], NT, preferred_element_type=f32) - sq_ref[...]
    old = top[...]
    new = jnp.maximum(old, jnp.max(logits, axis=1, keepdims=True))
    top[...] = new
    total[...] = total[...] * jnp.exp(old - new) + jnp.sum(
        jnp.exp(logits - new), axis=1, keepdims=True
    )

    @pl.when(step == pl.num_programs(0) - 1)
    def _():
        column = top[...] + jnp.log(total[...])
        lse[...] = column.reshape(1, 2 * half)


def stats_pass(first, second, words, sq, tile):
    half, depth = first.shape
    count = words.shape[0]
    return pl.pallas_call(
        stats_kernel,
        grid=(count // tile,),
        in_specs=[
            pl.BlockSpec((half, depth), lambda t: (0, 0)),
            pl.BlockSpec((half, depth), lambda t: (0, 0)),
            pl.BlockSpec((tile, depth), lambda t: (t, 0)),
            pl.BlockSpec((1, tile), lambda t: (0, t)),
        ],
        out_specs=pl.BlockSpec((1, 2 * half), lambda t: (0, 0)),
        out_shape=jax.ShapeDtypeStruct((1, 2 * half), f32),
        scratch_shapes=[
            pltpu.VMEM((2 * half, 1), f32),
            pltpu.VMEM((2 * half, 1), f32),
            pltpu.VMEM((2 * half, depth), bf16),
        ],
        name="stats_pass",
        cost_estimate=pl.CostEstimate(
            flops=4 * half * count * depth, bytes_accessed=2 * count * depth, transcendentals=0
        ),
        compiler_params=pltpu.CompilerParams(vmem_limit_bytes=24 * 2**20),
    )(first, second, words, sq)


def last_kernel(own, w_ref, r_ref, lse_ref, out, acc, counts, sq):
    step = pl.program_id(0)

    @pl.when(step == 0)
    def _():
        acc[...] = jnp.zeros_like(acc)
        counts[...] = jnp.zeros_like(counts)
        sq[...] = row_norms(w_ref[...])[:, None]

    words = w_ref[...]
    block = r_ref[...]
    logits = 2.0 * lax.dot_general(words, block, NT, preferred_element_type=f32)
    assign = jnp.exp(logits - sq[...] - lse_ref[...]).astype(bf16)
    acc[...] += lax.dot_general(assign, block, NN, preferred_element_type=f32)
    counts[...] += jnp.sum(assign.astype(f32), axis=1, keepdims=True)

    @pl.when(step == pl.num_programs(0) - 1)
    def _():
        out[...] = (acc[...] + smoothing * words.astype(f32)) / (counts[...] + smoothing)


def last_pass(own, words, block, lse, owned, tile):
    rows, depth = block.shape
    return pl.pallas_call(
        last_kernel,
        grid_spec=pltpu.PrefetchScalarGridSpec(
            num_scalar_prefetch=1,
            grid=(rows // tile,),
            in_specs=[
                pl.BlockSpec((owned, depth), lambda t, own: (own[0], 0)),
                pl.BlockSpec((tile, depth), lambda t, own: (t, 0)),
                pl.BlockSpec((1, tile), lambda t, own: (0, t)),
            ],
            out_specs=pl.BlockSpec((owned, depth), lambda t, own: (0, 0)),
            scratch_shapes=[
                pltpu.VMEM((owned, depth), f32),
                pltpu.VMEM((owned, 1), f32),
                pltpu.VMEM((owned, 1), f32),
            ],
        ),
        out_shape=jax.ShapeDtypeStruct((owned, depth), f32),
        name="last_pass",
        compiler_params=pltpu.CompilerParams(vmem_limit_bytes=32 * 2**20),
    )(own, words, block, lse)


def to_other(value, axis, flip):
    return lax.ppermute(value, axis, [(i, i ^ flip) for i in range(lax.axis_size(axis))])


def to_column(value, step):
    n = lax.axis_size("dp")
    table = []
    for book in range(2):
        for core in range(2):
            hop = n // 2 - 1 - step if core == 0 else step
            for d in range(n):
                here = (book * 2 + core) * n + d
                there = ((1 - book) * 2 + core) * n + (d ^ (2 * hop))
                table.append((here, there))
    return lax.ppermute(value, ("pair", "code", "dp"), table)


def shards(samples, codebooks):
    words = pltpu.with_memory_space_constraint(codebooks[0], pltpu.HBM)
    rows, depth = samples.shape
    half = rows // 2
    n = lax.axis_size("dp")
    core = lax.axis_index("code")
    mine, other, sq = first_pass(core.reshape(1), samples, words, 1024)
    theirs = to_other(other, "code", 1)

    def parts(value):
        return value[:, depth : depth + 1], value[:, depth + LANES : depth + LANES + 1], value[:, :depth]

    top_a, total_a, sum_a = parts(mine)
    top_b, total_b, sum_b = parts(theirs)
    top = jnp.maximum(top_a, top_b)
    scale_a, scale_b = jnp.exp(top_a - top), jnp.exp(top_b - top)
    rebuilt = (sum_a * scale_a + sum_b * scale_b) / (total_a * scale_a + total_b * scale_b)
    own_rows = lax.dynamic_slice_in_dim(samples, core * half, half, 0)
    residual = (own_rows.astype(f32) - rebuilt.astype(bf16).astype(f32)).astype(bf16)

    direct = [to_column(residual, i) for i in range(n // 2)]
    swapped = [to_other(value, "code", 1) for value in direct]
    lse = stats_pass(direct[0], swapped[0], words, sq, 1024)
    far = to_other(lse, "code", 1)
    far = jnp.concatenate([far[:, half:], far[:, :half]], axis=1)
    lse = jnp.logaddexp(lse, far)
    flip = 1
    while flip < n:
        lse = jnp.concatenate([lse, to_other(lse, "dp", flip)], axis=0)
        flip *= 2
    near = [to_other(value, "dp", 1) for value in direct]
    near_swapped = [to_other(value, "code", 1) for value in near]
    pieces = []
    for group in zip(direct, swapped, near, near_swapped):
        pieces += group
    everything = jnp.concatenate(pieces, axis=0)
    own = lax.axis_index("dp").reshape(1)
    updated = last_pass(
        own, words, everything, lse.reshape(1, n * rows), words.shape[0] // n, 2 * rows
    )
    return updated[None]


def solution(mesh):
    in_specs = (P("dp", None), P("pair", "code", None))
    out_specs = P("pair", ("code", "dp"), None)
    return jax.shard_map(shards, mesh=mesh, in_specs=in_specs, out_specs=out_specs, check_vma=False)
```

time: 656 us -> 99.9 us (0.15)
  waiting for transfers between devices: 490 us -> 18.8 us
  matrix products: 50.6 us -> 0 us
  blocking collectives: 50 us -> 0 us
  other arithmetic: 44.3 us -> 1.12 us
  Pallas kernels: 0 us -> 43.1 us
  starting transfers between devices: 2.87 us -> 29.3 us
  between operations: 14.8 us -> 0.22 us
    reduce_scatter x1 -> x0, waiting for transfers between devices: 480 us -> none  [shards(): lax.psum_scatter(partial_value, 'dp', scatter_dimension=0, tiled=True)]
    dot_general x4 -> x0, matrix products: 50.6 us -> none  [the longest x2 28.2 us: scores_of(): lax.dot_general(block, words, (((1,), (1,)), ((), ())), preferred_element...]
    pallas_call x0 -> x3, Pallas kernels: none -> 43.1 us  [the longest x1 16.1 us: first_pass(): pl.pallas_call(first_kernel, grid=(count // tile,), in_specs=[pl.BlockSpe...]
    unnamed x2 -> x0, blocking collectives: 42.6 us -> none
    ppermute x1 -> x21, starting transfers between devices: 2.87 us -> 29.3 us  [the longest x17 16.6 us: to_other(): lax.ppermute(value, axis, [(i, i ^ flip) for i in range(lax.axis_size(axi...]
    reduce_sum x4 -> x0, other arithmetic: 18.5 us -> none  [the longest x1 7.23 us: shards(): sq_norms = jnp.sum(words32 * words32, axis=-1)]
    convert_element_type x3 -> x1, other arithmetic: 18.9 us -> 0.85 us  [shards(): (own_rows.astype(f32) - rebuilt.astype(bf16).astype(f32)).astype(bf16)]
    ppermute x1 -> x21, waiting for transfers between devices: 9.45 us -> 18.8 us  [the longest x17 13.6 us: to_other(): lax.ppermute(value, axis, [(i, i ^ flip) for i in range(lax.axis_size(axi...]
  transfers between devices with their start and end apart: 2 -> 21, of which waited for: 2 -> 9; matrix products, arithmetic and copies ran while one was open for 3% -> 6% of each run, Pallas kernels for 0% -> 0%
where the time goes in v1:
time: 99.9 us; the launch traced here: 99.4 us
  Pallas kernels  43.1 us (43%)
  starting transfers between devices  29.3 us (29%)
  waiting for transfers between devices  18.8 us (19%)
  local copies, waits for them, and re-layouts  6.94 us (7%)
  other arithmetic  1.12 us (1%)
    ppermute x17, starting transfers between devices, to_other(): lax.ppermute(value, axis, [(i, i ^ flip) for i in range(lax.axis_size(axi...  16.6 us
    pallas_call x1, Pallas kernels, first_pass(): pl.pallas_call(first_kernel, grid=(count // tile,), in_specs=[pl.BlockSpe...  16.1 us
    pallas_call x1, Pallas kernels, last_pass(): pl.pallas_call(last_kernel, grid_spec=pltpu.PrefetchScalarGridSpec(num_sc...  14.5 us
    ppermute x17, waiting for transfers between devices, to_other(): lax.ppermute(value, axis, [(i, i ^ flip) for i in range(lax.axis_size(axi...  13.6 us
    ppermute x4, starting transfers between devices, to_column(): return lax.ppermute(value, ('pair', 'code', 'dp'), table)  12.6 us
    pallas_call x1, Pallas kernels, stats_pass(): pl.pallas_call(stats_kernel, grid=(count // tile,), in_specs=[pl.BlockSpe...  12.5 us
    unnamed x19, local copies, waits for them, and re-layouts  6.78 us
    ppermute x4, waiting for transfers between devices, to_column(): return lax.ppermute(value, ('pair', 'code', 'dp'), table)  5.18 us
  transfers between devices with their start and end apart: 21, of which 9 were waited for; matrix products, arithmetic and copies ran while one was open for 6% of the time, Pallas kernels for 0%

profile of v1, /device:TPU:0, one launch (start us, length us, event | category | flops | bytes accessed | tf_op | source)
XLA Modules:
  0.0 99.4 jit_solution(1426997350226407993)
XLA Ops:
  0.0 1.0 copy-done
  1.0 16.1 %first_pass.1 = (f32[96,1280]{1,0:T(8,128)S(1)}, f32[96,1280]{1,0:T(8,128)S(1)}, f32[1,8192]{1,0:T(1,128)S(1)}) custom-call(s32[1]{0:T(128)} %bitcast.2.core, bf16[192,1024]{1,0:T(8,128)(2,1)S(1)} %copy-done, bf16[8192,1024]{1,0:T(8,128)(2,1)} %bitcast.4), custom_call_target="tpu_custom_call" | custom-call | tf_op jit(solution)/shard_map/first_pass/pallas_call | solution.py:71
  17.1 0.6 collective-permute-start
  17.6 1.5 %collective-permute-done = f32[96,1280]{1,0:T(8,128)S(1)} collective-permute-done((f32[96,1280]{1,0:T(8,128)S(1)}, f32[96,1280]{1,0:T(8,128)S(1)}, u32[]{:S(2)}, u32[]{:S(2)}) %collective-permute-start) | collective-permute-done | bytes 491552 | tf_op jit(solution)/shard_map/ppermute | solution.py:192
  19.3 0.9 subtract_convert_fusion
  20.1 5.9 %collective-permute-start.1 = (bf16[96,1024]{1,0:T(8,128)(2,1)}, bf16[96,1024]{1,0:T(8,128)(2,1)S(1)}, u32[]{:S(2)}, u32[]{:S(2)}) collective-permute-start(bf16[96,1024]{1,0:T(8,128)(2,1)} %subtract_convert_fusion), channel_id=1, source_target_pairs={{0,22},{1,23},{2,20},{3,21},{4,18},{5,19},{6,16},{7,17},{8,24},{9,... | collective-permute-start | bytes 589832 | tf_op jit(solution)/shard_map/ppermute | solution.py:205
  26.1 4.0 %collective-permute-done.1.a_ref = bf16[96,1024]{1,0:T(8,128)(2,1)S(1)} collective-permute-done((bf16[96,1024]{1,0:T(8,128)(2,1)}, bf16[96,1024]{1,0:T(8,128)(2,1)S(1)}, u32[]{:S(2)}, u32[]{:S(2)}) %collective-permute-start.1) | collective-permute-done | bytes 196640 | tf_op jit(solution)/shard_map/ppermute | solution.py:205
  30.0 1.4 %collective-permute-done.2.b_ref = bf16[96,1024]{1,0:T(8,128)(2,1)S(1)} collective-permute-done((bf16[96,1024]{1,0:T(8,128)(2,1)S(1)}, bf16[96,1024]{1,0:T(8,128)(2,1)S(1)}, u32[]{:S(2)}, u32[]{:S(2)}) %collective-permute-start.2) | collective-permute-done | bytes 196640 | tf_op jit(solution)/shard_map/ppermute | solution.py:192
  31.5 12.5 %stats_pass.1 = f32[1,192]{1,0:T(1,128)S(1)} custom-call(bf16[96,1024]{1,0:T(8,128)(2,1)S(1)} %collective-permute-done.1.a_ref, bf16[96,1024]{1,0:T(8,128)(2,1)S(1)} %collective-permute-done.2.b_ref, bf16[8192,1024]{1,0:T(8,128)(2,1)} %bitcast.5, f32[1,8192]{1,0:T(1,128)S(1)} %get-tuple-element.10.sq_ref), custom_call_target="tpu_custom_call" | custom-call | flops 3221225472 | bytes 16777216 | tf_op jit(solution)/shard_map/stats_pass/pallas_call | solution.py:121
  44.2 4.0 %collective-permute-start.5 = (bf16[96,1024]{1,0:T(8,128)(2,1)}, bf16[96,1024]{1,0:T(8,128)(2,1)}, u32[]{:S(2)}, u32[]{:S(2)}) collective-permute-start(bf16[96,1024]{1,0:T(8,128)(2,1)} %subtract_convert_fusion), channel_id=1, source_target_pairs={{0,20},{1,21},{2,22},{3,23},{4,16},{5,17},{6,18},{7,19},{8,26},{9,... | collective-permute-start | bytes 589832 | tf_op jit(solution)/shard_map/ppermute | solution.py:205
  48.1 1.3 %collective-permute-start.9 = (bf16[96,1024]{1,0:T(8,128)(2,1)}, bf16[96,1024]{1,0:T(8,128)(2,1)}, u32[]{:S(2)}, u32[]{:S(2)}) collective-permute-start(bf16[96,1024]{1,0:T(8,128)(2,1)} %subtract_convert_fusion), channel_id=1, source_target_pairs={{0,18},{1,19},{2,16},{3,17},{4,22},{5,23},{6,20},{7,21},{8,28},{9,... | collective-permute-start | bytes 589832 | tf_op jit(solution)/shard_map/ppermute | solution.py:205
  49.4 1.5 %collective-permute-start.13 = (bf16[96,1024]{1,0:T(8,128)(2,1)}, bf16[96,1024]{1,0:T(8,128)(2,1)}, u32[]{:S(2)}, u32[]{:S(2)}) collective-permute-start(bf16[96,1024]{1,0:T(8,128)(2,1)} %subtract_convert_fusion), channel_id=1, source_target_pairs={{0,16},{1,17},{2,18},{3,19},{4,20},{5,21},{6,22},{7,23},{8,30},{9,... | collective-permute-start | bytes 589832 | tf_op jit(solution)/shard_map/ppermute | solution.py:205
  51.1 1.6 %collective-permute-start.18 = (f32[1,192]{1,0:T(1,128)S(1)}, f32[1,192]{1,0:T(1,128)S(1)}, u32[]{:S(2)}, u32[]{:S(2)}) collective-permute-start(f32[1,192]{1,0:T(1,128)S(1)} %compare_select_fusion), channel_id=1, source_target_pairs={{0,1},{1,0},{2,3},{3,2},{4,5},{5,4},{6,7},{7,6},{8,9},{9,8},{10,11... | collective-permute-start | bytes 2312 | tf_op jit(solution)/shard_map/ppermute | solution.py:192
  52.7 0.6 collective-permute-start.3
  53.3 1.2 %collective-permute-done.5 = bf16[96,1024]{1,0:T(8,128)(2,1)} collective-permute-done((bf16[96,1024]{1,0:T(8,128)(2,1)}, bf16[96,1024]{1,0:T(8,128)(2,1)}, u32[]{:S(2)}, u32[]{:S(2)}) %collective-permute-start.5) | collective-permute-done | bytes 196640 | tf_op jit(solution)/shard_map/ppermute | solution.py:205
  54.7 6.6 %collective-permute-start.19 = (f32[2,192]{1,0:T(2,128)S(1)}, f32[2,192]{1,0:T(2,128)S(1)}, u32[]{:S(2)}, u32[]{:S(2)}) collective-permute-start(f32[2,192]{1,0:T(2,128)S(1)} %pad_maximum_fusion.2), channel_id=1, source_target_pairs={{0,2},{1,3},{2,0},{3,1},{4,6},{5,7},{6,4},{7,5},{8,10},{9,11},{10,... | collective-permute-start | bytes 4616 | tf_op jit(solution)/shard_map/ppermute | solution.py:192
  61.3 0.3 collective-permute-start.4
  61.6 1.2 %collective-permute-done.19 = f32[2,192]{1,0:T(2,128)S(1)} collective-permute-done((f32[2,192]{1,0:T(2,128)S(1)}, f32[2,192]{1,0:T(2,128)S(1)}, u32[]{:S(2)}, u32[]{:S(2)}) %collective-permute-start.19) | collective-permute-done | bytes 1568 | tf_op jit(solution)/shard_map/ppermute | solution.py:192
  62.9 3.1 %collective-permute-start.20 = (f32[4,192]{1,0:T(4,128)S(1)}, f32[4,192]{1,0:T(4,128)S(1)}, u32[]{:S(2)}, u32[]{:S(2)}) collective-permute-start(f32[4,192]{1,0:T(4,128)S(1)} %pad_maximum_fusion.1), channel_id=1, source_target_pairs={{0,4},{1,5},{2,6},{3,7},{4,0},{5,1},{6,2},{7,3},{8,12},{9,13},{10,... | collective-permute-start | bytes 9224 | tf_op jit(solution)/shard_map/ppermute | solution.py:192
  66.0 0.9 constant_dynamic-update-slice_fusion.13
  66.9 1.6 %collective-permute-start.7 = (bf16[96,1024]{1,0:T(8,128)(2,1)}, bf16[96,1024]{1,0:T(8,128)(2,1)S(1)}, u32[]{:S(2)}, u32[]{:S(2)}) collective-permute-start(bf16[96,1024]{1,0:T(8,128)(2,1)} %collective-permute-done.5), channel_id=1, source_target_pairs={{0,1},{1,0},{2,3},{3,2},{4,5},{5,4},{6,7},{7,6},{8,9},{9,8},{10,11... | collective-permute-start | bytes 589832 | tf_op jit(solution)/shard_map/ppermute | solution.py:192
  68.6 0.6 collective-permute-start.11
  69.3 1.4 %collective-permute-start.15 = (bf16[96,1024]{1,0:T(8,128)(2,1)}, bf16[96,1024]{1,0:T(8,128)(2,1)S(1)}, u32[]{:S(2)}, u32[]{:S(2)}) collective-permute-start(bf16[96,1024]{1,0:T(8,128)(2,1)} %collective-permute-done.13), channel_id=1, source_target_pairs={{0,1},{1,0},{2,3},{3,2},{4,5},{5,4},{6,7},{7,6},{8,9},{9,8},{10,11... | collective-permute-start | bytes 589832 | tf_op jit(solution)/shard_map/ppermute | solution.py:192
  70.7 0.9 constant_dynamic-update-slice_fusion.12
  71.6 0.9 constant_dynamic-update-slice_fusion.11
  72.7 2.1 %collective-permute-done.7 = bf16[96,1024]{1,0:T(8,128)(2,1)S(1)} collective-permute-done((bf16[96,1024]{1,0:T(8,128)(2,1)}, bf16[96,1024]{1,0:T(8,128)(2,1)S(1)}, u32[]{:S(2)}, u32[]{:S(2)}) %collective-permute-start.7) | collective-permute-done | bytes 196640 | tf_op jit(solution)/shard_map/ppermute | solution.py:192
  74.8 4.2 %collective-permute-done.11 = bf16[96,1024]{1,0:T(8,128)(2,1)S(1)} collective-permute-done((bf16[96,1024]{1,0:T(8,128)(2,1)}, bf16[96,1024]{1,0:T(8,128)(2,1)S(1)}, u32[]{:S(2)}, u32[]{:S(2)}) %collective-permute-start.11) | collective-permute-done | bytes 196640 | tf_op jit(solution)/shard_map/ppermute | solution.py:192
  79.0 2.8 %collective-permute-done.15 = bf16[96,1024]{1,0:T(8,128)(2,1)S(1)} collective-permute-done((bf16[96,1024]{1,0:T(8,128)(2,1)}, bf16[96,1024]{1,0:T(8,128)(2,1)S(1)}, u32[]{:S(2)}, u32[]{:S(2)}) %collective-permute-start.15) | collective-permute-done | bytes 196640 | tf_op jit(solution)/shard_map/ppermute | solution.py:192
  81.8 0.9 constant_dynamic-update-slice_fusion.10
  82.8 0.9 constant_dynamic-update-slice_fusion.7
  83.9 0.9 constant_dynamic-update-slice_fusion.3
  84.9 14.5 %last_pass.1 = f32[1024,1024]{1,0:T(8,128)} custom-call(s32[1]{0:T(128)} %bitcast.own, bf16[8192,1024]{1,0:T(8,128)(2,1)} %bitcast.6, bf16[1536,1024]{1,0:T(8,128)(2,1)S(1)} %constant_dynamic-update-slice_fusion.r_ref, f32[1,1536]{1,0:T(1,128)S(1)} %reshape.11.lse_ref), custom_call_target="tpu_custom_call" | custom-call | tf_op jit(solution)/shard_map/last_pass/pallas_call | solution.py:168
  (41 shorter events, 1.2 us)
Async XLA Ops:
  0.0 1.0 %copy-start = (bf16[192,1024]{1,0:T(8,128)(2,1)S(1)}, bf16[192,1024]{1,0:T(8,128)(2,1)}, u32[]{:S(2)}) copy-start(bf16[192,1024]{1,0:T(8,128)(2,1)} %s_ref.1) | copy-start | bytes 1179652
  1.0 18.3 %copy-start.1 = (bf16[192,1024]{1,0:T(8,128)(2,1)S(1)}, bf16[192,1024]{1,0:T(8,128)(2,1)}, u32[]{:S(2)}) copy-start(bf16[192,1024]{1,0:T(8,128)(2,1)} %s_ref.1) | copy-start | bytes 1179652
  17.1 2.0 %collective-permute-start = (f32[96,1280]{1,0:T(8,128)S(1)}, f32[96,1280]{1,0:T(8,128)S(1)}, u32[]{:S(2)}, u32[]{:S(2)}) collective-permute-start(f32[96,1280]{1,0:T(8,128)S(1)} %get-tuple-element.9), channel_id=1, source_target_pairs={{0,8},{8,0},{1,9},{9,1},{2,10},{10,2},{3,11},{11,3},{4,12},{12,4},... | collective-permute-start | bytes 1474568 | tf_op jit(solution)/shard_map/ppermute | solution.py:192
  20.1 9.9 %collective-permute-start.1 = (bf16[96,1024]{1,0:T(8,128)(2,1)}, bf16[96,1024]{1,0:T(8,128)(2,1)S(1)}, u32[]{:S(2)}, u32[]{:S(2)}) collective-permute-start(bf16[96,1024]{1,0:T(8,128)(2,1)} %subtract_convert_fusion), channel_id=1, source_target_pairs={{0,22},{1,23},{2,20},{3,21},{4,18},{5,19},{6,16},{7,17},{8,24},{9,... | collective-permute-start | bytes 589832 | tf_op jit(solution)/shard_map/ppermute | solution.py:205
  30.0 1.4 %collective-permute-start.2 = (bf16[96,1024]{1,0:T(8,128)(2,1)S(1)}, bf16[96,1024]{1,0:T(8,128)(2,1)S(1)}, u32[]{:S(2)}, u32[]{:S(2)}) collective-permute-start(bf16[96,1024]{1,0:T(8,128)(2,1)S(1)} %collective-permute-done.1.a_ref), channel_id=1, source_target_pairs={{0,8},{8,0},{1,9},{9,1},{2,10},{10,2},{3,11},{11,3},{4,12},{12,4},... | collective-permute-start | bytes 589832 | tf_op jit(solution)/shard_map/ppermute | solution.py:192
  44.0 7.0 %collective-permute-start.17 = (f32[1,192]{1,0:T(1,128)S(1)}, f32[1,192]{1,0:T(1,128)S(1)}, u32[]{:S(2)}, u32[]{:S(2)}) collective-permute-start(f32[1,192]{1,0:T(1,128)S(1)} %stats_pass.1), channel_id=1, source_target_pairs={{0,8},{8,0},{1,9},{9,1},{2,10},{10,2},{3,11},{11,3},{4,12},{12,4},... | collective-permute-start | bytes 2312 | tf_op jit(solution)/shard_map/ppermute | solution.py:192
  44.2 10.3 %collective-permute-start.5 = (bf16[96,1024]{1,0:T(8,128)(2,1)}, bf16[96,1024]{1,0:T(8,128)(2,1)}, u32[]{:S(2)}, u32[]{:S(2)}) collective-permute-start(bf16[96,1024]{1,0:T(8,128)(2,1)} %subtract_convert_fusion), channel_id=1, source_target_pairs={{0,20},{1,21},{2,22},{3,23},{4,16},{5,17},{6,18},{7,19},{8,26},{9,... | collective-permute-start | bytes 589832 | tf_op jit(solution)/shard_map/ppermute | solution.py:205
  48.1 18.8 %collective-permute-start.9 = (bf16[96,1024]{1,0:T(8,128)(2,1)}, bf16[96,1024]{1,0:T(8,128)(2,1)}, u32[]{:S(2)}, u32[]{:S(2)}) collective-permute-start(bf16[96,1024]{1,0:T(8,128)(2,1)} %subtract_convert_fusion), channel_id=1, source_target_pairs={{0,18},{1,19},{2,16},{3,17},{4,22},{5,23},{6,20},{7,21},{8,28},{9,... | collective-permute-start | bytes 589832 | tf_op jit(solution)/shard_map/ppermute | solution.py:205
  49.4 19.2 %collective-permute-start.13 = (bf16[96,1024]{1,0:T(8,128)(2,1)}, bf16[96,1024]{1,0:T(8,128)(2,1)}, u32[]{:S(2)}, u32[]{:S(2)}) collective-permute-start(bf16[96,1024]{1,0:T(8,128)(2,1)} %subtract_convert_fusion), channel_id=1, source_target_pairs={{0,16},{1,17},{2,18},{3,19},{4,20},{5,21},{6,22},{7,23},{8,30},{9,... | collective-permute-start | bytes 589832 | tf_op jit(solution)/shard_map/ppermute | solution.py:205
  51.1 3.7 %collective-permute-start.18 = (f32[1,192]{1,0:T(1,128)S(1)}, f32[1,192]{1,0:T(1,128)S(1)}, u32[]{:S(2)}, u32[]{:S(2)}) collective-permute-start(f32[1,192]{1,0:T(1,128)S(1)} %compare_select_fusion), channel_id=1, source_target_pairs={{0,1},{1,0},{2,3},{3,2},{4,5},{5,4},{6,7},{7,6},{8,9},{9,8},{10,11... | collective-permute-start | bytes 2312 | tf_op jit(solution)/shard_map/ppermute | solution.py:192
  52.7 8.7 %collective-permute-start.3 = (bf16[96,1024]{1,0:T(8,128)(2,1)S(1)}, bf16[96,1024]{1,0:T(8,128)(2,1)}, u32[]{:S(2)}, u32[]{:S(2)}) collective-permute-start(bf16[96,1024]{1,0:T(8,128)(2,1)S(1)} %collective-permute-done.1.a_ref), channel_id=1, source_target_pairs={{0,1},{1,0},{2,3},{3,2},{4,5},{5,4},{6,7},{7,6},{8,9},{9,8},{10,11... | collective-permute-start | bytes 589832 | tf_op jit(solution)/shard_map/ppermute | solution.py:192
  54.5 18.1 %collective-permute-start.6 = (bf16[96,1024]{1,0:T(8,128)(2,1)}, bf16[96,1024]{1,0:T(8,128)(2,1)}, u32[]{:S(2)}, u32[]{:S(2)}) collective-permute-start(bf16[96,1024]{1,0:T(8,128)(2,1)} %collective-permute-done.5), channel_id=1, source_target_pairs={{0,8},{8,0},{1,9},{9,1},{2,10},{10,2},{3,11},{11,3},{4,12},{12,4},... | collective-permute-start | bytes 589832 | tf_op jit(solution)/shard_map/ppermute | solution.py:192
  54.7 8.1 %collective-permute-start.19 = (f32[2,192]{1,0:T(2,128)S(1)}, f32[2,192]{1,0:T(2,128)S(1)}, u32[]{:S(2)}, u32[]{:S(2)}) collective-permute-start(f32[2,192]{1,0:T(2,128)S(1)} %pad_maximum_fusion.2), channel_id=1, source_target_pairs={{0,2},{1,3},{2,0},{3,1},{4,6},{5,7},{6,4},{7,5},{8,10},{9,11},{10,... | collective-permute-start | bytes 4616 | tf_op jit(solution)/shard_map/ppermute | solution.py:192
  61.3 7.9 %collective-permute-start.4 = (bf16[96,1024]{1,0:T(8,128)(2,1)}, bf16[96,1024]{1,0:T(8,128)(2,1)}, u32[]{:S(2)}, u32[]{:S(2)}) collective-permute-start(bf16[96,1024]{1,0:T(8,128)(2,1)} %collective-permute-done.3), channel_id=1, source_target_pairs={{0,8},{8,0},{1,9},{9,1},{2,10},{10,2},{3,11},{11,3},{4,12},{12,4},... | collective-permute-start | bytes 589832 | tf_op jit(solution)/shard_map/ppermute | solution.py:192
  62.9 5.6 %collective-permute-start.20 = (f32[4,192]{1,0:T(4,128)S(1)}, f32[4,192]{1,0:T(4,128)S(1)}, u32[]{:S(2)}, u32[]{:S(2)}) collective-permute-start(f32[4,192]{1,0:T(4,128)S(1)} %pad_maximum_fusion.1), channel_id=1, source_target_pairs={{0,4},{1,5},{2,6},{3,7},{4,0},{5,1},{6,2},{7,3},{8,12},{9,13},{10,... | collective-permute-start | bytes 9224 | tf_op jit(solution)/shard_map/ppermute | solution.py:192
  66.9 7.8 %collective-permute-start.7 = (bf16[96,1024]{1,0:T(8,128)(2,1)}, bf16[96,1024]{1,0:T(8,128)(2,1)S(1)}, u32[]{:S(2)}, u32[]{:S(2)}) collective-permute-start(bf16[96,1024]{1,0:T(8,128)(2,1)} %collective-permute-done.5), channel_id=1, source_target_pairs={{0,1},{1,0},{2,3},{3,2},{4,5},{5,4},{6,7},{7,6},{8,9},{9,8},{10,11... | collective-permute-start | bytes 589832 | tf_op jit(solution)/shard_map/ppermute | solution.py:192
  68.5 15.2 %collective-permute-start.10 = (bf16[96,1024]{1,0:T(8,128)(2,1)}, bf16[96,1024]{1,0:T(8,128)(2,1)S(1)}, u32[]{:S(2)}, u32[]{:S(2)}) collective-permute-start(bf16[96,1024]{1,0:T(8,128)(2,1)} %collective-permute-done.9), channel_id=1, source_target_pairs={{0,8},{8,0},{1,9},{9,1},{2,10},{10,2},{3,11},{11,3},{4,12},{12,4},... | collective-permute-start | bytes 589832 | tf_op jit(solution)/shard_map/ppermute | solution.py:192
  68.6 10.4 %collective-permute-start.11 = (bf16[96,1024]{1,0:T(8,128)(2,1)}, bf16[96,1024]{1,0:T(8,128)(2,1)S(1)}, u32[]{:S(2)}, u32[]{:S(2)}) collective-permute-start(bf16[96,1024]{1,0:T(8,128)(2,1)} %collective-permute-done.9), channel_id=1, source_target_pairs={{0,1},{1,0},{2,3},{3,2},{4,5},{5,4},{6,7},{7,6},{8,9},{9,8},{10,11... | collective-permute-start | bytes 589832 | tf_op jit(solution)/shard_map/ppermute | solution.py:192
  69.3 12.5 %collective-permute-start.15 = (bf16[96,1024]{1,0:T(8,128)(2,1)}, bf16[96,1024]{1,0:T(8,128)(2,1)S(1)}, u32[]{:S(2)}, u32[]{:S(2)}) collective-permute-start(bf16[96,1024]{1,0:T(8,128)(2,1)} %collective-permute-done.13), channel_id=1, source_target_pairs={{0,1},{1,0},{2,3},{3,2},{4,5},{5,4},{6,7},{7,6},{8,9},{9,8},{10,11... | collective-permute-start | bytes 589832 | tf_op jit(solution)/shard_map/ppermute | solution.py:192
  72.6 12.2 %collective-permute-start.14 = (bf16[96,1024]{1,0:T(8,128)(2,1)}, bf16[96,1024]{1,0:T(8,128)(2,1)S(1)}, u32[]{:S(2)}, u32[]{:S(2)}) collective-permute-start(bf16[96,1024]{1,0:T(8,128)(2,1)} %collective-permute-done.13), channel_id=1, source_target_pairs={{0,8},{8,0},{1,9},{9,1},{2,10},{10,2},{3,11},{11,3},{4,12},{12,4},... | collective-permute-start | bytes 589832 | tf_op jit(solution)/shard_map/ppermute | solution.py:192
  74.8 8.0 %collective-permute-start.8 = (bf16[96,1024]{1,0:T(8,128)(2,1)S(1)}, bf16[96,1024]{1,0:T(8,128)(2,1)S(1)}, u32[]{:S(2)}, u32[]{:S(2)}) collective-permute-start(bf16[96,1024]{1,0:T(8,128)(2,1)S(1)} %collective-permute-done.7), channel_id=1, source_target_pairs={{0,8},{8,0},{1,9},{9,1},{2,10},{10,2},{3,11},{11,3},{4,12},{12,4},... | collective-permute-start | bytes 589832 | tf_op jit(solution)/shard_map/ppermute | solution.py:192
  79.0 4.8 %collective-permute-start.12 = (bf16[96,1024]{1,0:T(8,128)(2,1)S(1)}, bf16[96,1024]{1,0:T(8,128)(2,1)S(1)}, u32[]{:S(2)}, u32[]{:S(2)}) collective-permute-start(bf16[96,1024]{1,0:T(8,128)(2,1)S(1)} %collective-permute-done.11), channel_id=1, source_target_pairs={{0,8},{8,0},{1,9},{9,1},{2,10},{10,2},{3,11},{11,3},{4,12},{12,4},... | collective-permute-start | bytes 589832 | tf_op jit(solution)/shard_map/ppermute | solution.py:192
  81.8 3.0 %collective-permute-start.16 = (bf16[96,1024]{1,0:T(8,128)(2,1)S(1)}, bf16[96,1024]{1,0:T(8,128)(2,1)S(1)}, u32[]{:S(2)}, u32[]{:S(2)}) collective-permute-start(bf16[96,1024]{1,0:T(8,128)(2,1)S(1)} %collective-permute-done.15), channel_id=1, source_target_pairs={{0,8},{8,0},{1,9},{9,1},{2,10},{10,2},{3,11},{11,3},{4,12},{12,4},... | collective-permute-start | bytes 589832 | tf_op jit(solution)/shard_map/ppermute | solution.py:192

commit v2 on v0

v2 whole, which is shorter than its diff:
```python
import functools

import jax
import jax.numpy as jnp
from jax import lax
from jax.experimental import pallas as pl
from jax.experimental.pallas import tpu as pltpu
from jax.sharding import PartitionSpec as P


smoothing = 0.5
f32, bf16 = jnp.float32, jnp.bfloat16
NT = (((1,), (1,)), ((), ()))
NN = (((1,), (0,)), ((), ()))
TN = (((0,), (0,)), ((), ()))
LANES = 128
SUBLANES = 8
AHEAD = 2
VMEM = pl.BlockSpec(memory_space=pltpu.VMEM)
SMEM = pl.BlockSpec(memory_space=pltpu.SMEM)
HBM = pl.BlockSpec(memory_space=pltpu.HBM)


def square_sums(words):
    wide = words.astype(f32)
    return jnp.sum(wide * wide, axis=1, keepdims=True)


def span(t, tile):
    return pl.ds(pl.multiple_of(t * tile, tile), tile)


def tile_copy(source, held, sems, tile, t):
    at = span(t, tile)
    return pltpu.make_async_copy(source.at[at], held.at[at], sems.at[t])


def first_kernel(tile, core, s_hbm, w_hbm, mine, other, held, acc, top, twice, logits, sems, own_sem):
    rows, depth = twice.shape
    steps = w_hbm.shape[0] // tile
    fetch = pltpu.make_async_copy(s_hbm, twice, own_sem.at[0])
    fetch.start()
    for t in range(min(AHEAD, steps)):
        tile_copy(w_hbm, held, sems, tile, t).start()
    fetch.wait()
    twice[...] = twice[...] * 2
    top[...] = jnp.full_like(top, -jnp.inf)

    @pl.loop(0, steps)
    def _(t):
        @pl.when(t + AHEAD < steps)
        def _():
            tile_copy(w_hbm, held, sems, tile, t + AHEAD).start()

        tile_copy(w_hbm, held, sems, tile, t).wait()
        words = held[span(t, tile)]
        score = lax.dot_general(words, twice[...], NT, preferred_element_type=f32)
        score = score - square_sums(words)
        logits[span(t, tile)] = score
        groups = score.reshape(tile // SUBLANES, SUBLANES, rows)
        top[...] = jnp.maximum(top[...], jnp.max(groups, axis=0))

    best = jnp.max(top[...], axis=0, keepdims=True)
    acc[...] = jnp.zeros_like(acc)

    def add(t, total):
        expd = jnp.exp(logits[span(t, tile)] - best)
        acc[...] += lax.dot_general(
            expd.astype(bf16), held[span(t, tile)], TN, preferred_element_type=f32
        )
        return total + jnp.sum(expd.reshape(tile // SUBLANES, SUBLANES, rows), axis=0)

    total = lax.fori_loop(0, steps, add, jnp.zeros((SUBLANES, rows), f32))
    total = jnp.sum(total, axis=0, keepdims=True)
    tops = jnp.broadcast_to(best.reshape(rows, 1), (rows, LANES))
    totals = jnp.broadcast_to(total.reshape(rows, 1), (rows, LANES))
    half = rows // 2

    def put(ref, lo):
        at = slice(lo, lo + half)
        ref[:, :depth] = acc[at]
        ref[:, depth : depth + LANES] = tops[at]
        ref[:, depth + LANES :] = totals[at]

    @pl.when(core[0] == 0)
    def _():
        put(mine, 0)
        put(other, half)

    @pl.when(core[0] == 1)
    def _():
        put(mine, half)
        put(other, 0)


def first_pass(core, samples, words, tile):
    rows, depth = samples.shape
    count = words.shape[0]
    half = jax.ShapeDtypeStruct((rows // 2, depth + 2 * LANES), f32)
    return pl.pallas_call(
        functools.partial(first_kernel, tile),
        in_specs=[SMEM, HBM, HBM],
        out_specs=[VMEM, VMEM],
        out_shape=[half, half],
        scratch_shapes=[
            pltpu.VMEM((count, depth), bf16),
            pltpu.VMEM((rows, depth), f32),
            pltpu.VMEM((SUBLANES, rows), f32),
            pltpu.VMEM((rows, depth), bf16),
            pltpu.VMEM((count, rows), f32),
            pltpu.SemaphoreType.DMA((count // tile,)),
            pltpu.SemaphoreType.DMA((1,)),
        ],
        name="first_pass",
        compiler_params=pltpu.CompilerParams(vmem_limit_bytes=40 * 2**20),
    )(core, samples, words)


def join(core, samples, mine, theirs):
    half, depth = samples.shape[0] // 2, samples.shape[1]

    def parts(value):
        return value[:, depth : depth + 1], value[:, depth + LANES : depth + LANES + 1], value[:, :depth]

    top_a, total_a, sum_a = parts(mine)
    top_b, total_b, sum_b = parts(theirs)
    top = jnp.maximum(top_a, top_b)
    scale_a, scale_b = jnp.exp(top_a - top), jnp.exp(top_b - top)
    rebuilt = (sum_a * scale_a + sum_b * scale_b) / (total_a * scale_a + total_b * scale_b)
    own = lax.dynamic_slice_in_dim(samples, core[0] * half, half, 0)
    return (own.astype(f32) - rebuilt.astype(bf16).astype(f32)).astype(bf16)


def stats_kernel(tile, a_hbm, b_hbm, w_hbm, lse, held, top, total, twice, sems, row_sems):
    half = a_hbm.shape[0]
    steps = held.shape[0] // tile
    fetches = [
        pltpu.make_async_copy(source, twice.at[pl.ds(i * half, half)], row_sems.at[i])
        for i, source in enumerate((a_hbm, b_hbm))
    ]
    for fetch in fetches:
        fetch.start()
    for t in range(min(AHEAD, steps)):
        tile_copy(w_hbm, held, sems, tile, t).start()
    for fetch in fetches:
        fetch.wait()
    twice[...] = twice[...] * 2
    top[...] = jnp.full_like(top, -jnp.inf)
    total[...] = jnp.zeros_like(total)

    @pl.loop(0, steps)
    def _(t):
        @pl.when(t + AHEAD < steps)
        def _():
            tile_copy(w_hbm, held, sems, tile, t + AHEAD).start()

        tile_copy(w_hbm, held, sems, tile, t).wait()
        words = held[span(t, tile)]
        score = lax.dot_general(words, twice[...], NT, preferred_element_type=f32)
        score = (score - square_sums(words)).reshape(tile // SUBLANES, SUBLANES, 2 * half)
        old = top[...]
        new = jnp.maximum(old, jnp.max(score, axis=0))
        total[...] = total[...] * jnp.exp(old - new) + jnp.sum(jnp.exp(score - new[None]), axis=0)
        top[...] = new

    best = jnp.max(top[...], axis=0, keepdims=True)
    lse[...] = best + jnp.log(jnp.sum(total[...] * jnp.exp(top[...] - best), axis=0, keepdims=True))


def stats_pass(first, second, words, tile):
    half, depth = first.shape
    count = words.shape[0]
    return pl.pallas_call(
        functools.partial(stats_kernel, tile),
        in_specs=[HBM, HBM, HBM],
        out_specs=VMEM,
        out_shape=jax.ShapeDtypeStruct((1, 2 * half), f32),
        scratch_shapes=[
            pltpu.VMEM((count, depth), bf16),
            pltpu.VMEM((SUBLANES, 2 * half), f32),
            pltpu.VMEM((SUBLANES, 2 * half), f32),
            pltpu.VMEM((2 * half, depth), bf16),
            pltpu.SemaphoreType.DMA((count // tile,)),
            pltpu.SemaphoreType.DMA((2,)),
        ],
        name="stats_pass",
        cost_estimate=pl.CostEstimate(
            flops=4 * half * count * depth, bytes_accessed=2 * count * depth, transcendentals=0
        ),
        compiler_params=pltpu.CompilerParams(vmem_limit_bytes=60 * 2**20),
    )(first, second, words)


def row_fetches(pieces, block, sems, first):
    fetches, at = [], 0
    for i, piece in enumerate(pieces):
        rows = piece.shape[0]
        fetches.append(pltpu.make_async_copy(piece, block.at[pl.ds(at, rows)], sems.at[first + i]))
        at += rows
    return fetches


def score_kernel(count, own, w_hbm, *refs):
    pieces, (logits, block, words, sems) = refs[:count], refs[count:]
    fetch = pltpu.make_async_copy(w_hbm.at[span(own[0], words.shape[0])], words, sems.at[count])
    fetch.start()
    fetches = row_fetches(pieces, block, sems, 0)
    for other in fetches:
        other.start()
    fetch.wait()
    sq = square_sums(words[...])
    for other in fetches:
        other.wait()
    score = lax.dot_general(words[...] * 2, block[...], NT, preferred_element_type=f32)
    logits[...] = score - sq


def score_pass(own, words, pieces, owned):
    depth = words.shape[1]
    rows = sum(piece.shape[0] for piece in pieces)
    return pl.pallas_call(
        functools.partial(score_kernel, len(pieces)),
        in_specs=[SMEM, HBM] + [HBM] * len(pieces),
        out_specs=VMEM,
        scratch_shapes=[
            pltpu.VMEM((rows, depth), bf16),
            pltpu.VMEM((owned, depth), bf16),
            pltpu.SemaphoreType.DMA((len(pieces) + 1,)),
        ],
        out_shape=jax.ShapeDtypeStruct((owned, rows), f32),
        name="score_pass",
        cost_estimate=pl.CostEstimate(
            flops=2 * owned * rows * depth, bytes_accessed=2 * rows * depth, transcendentals=0
        ),
        compiler_params=pltpu.CompilerParams(vmem_limit_bytes=40 * 2**20),
    )(own, words, *pieces)


def last_kernel(count, tile, chunk, own, w_hbm, la_ref, lse_ref, *refs):
    near, direct = refs[:count], refs[count : 2 * count]
    out, block, words, assign, staged, sems, out_sems = refs[2 * count :]
    owned = words.shape[0]
    rows = la_ref.shape[1]
    fetch = pltpu.make_async_copy(w_hbm.at[span(own[0], owned)], words, sems.at[2 * count])
    fetch.start()
    fetches = row_fetches(near, block.at[pl.ds(rows, rows)], sems, 0)
    fetches += row_fetches(direct, block.at[pl.ds(0, rows)], sems, count)
    for other in fetches:
        other.start()
    assign[:, :rows] = jnp.exp(la_ref[...] - lse_ref[0:1]).astype(bf16)
    fetch.wait()
    sq = square_sums(words[...])
    twice = words[...] * 2
    each = near[0].shape[0]
    for lo in range(0, rows, chunk):
        for other in fetches[lo // each : (lo + chunk) // each]:
            other.wait()
        at = slice(rows + lo, rows + lo + chunk)
        score = lax.dot_general(twice, block[at], NT, preferred_element_type=f32)
        assign[:, at] = jnp.exp(score - sq - lse_ref[1:2, lo : lo + chunk]).astype(bf16)
    for other in fetches[count:]:
        other.wait()
    sends = []
    for lo in range(0, owned, tile):
        at = slice(lo, lo + tile)
        sums = lax.dot_general(assign[at], block[...], NN, preferred_element_type=f32)
        counts = jnp.sum(assign[at].astype(f32), axis=1, keepdims=True)
        staged[at] = (sums + smoothing * words[at].astype(f32)) / (counts + smoothing)
        sends.append(pltpu.make_async_copy(staged.at[at], out.at[at], out_sems.at[lo // tile]))
        sends[-1].start()
    for send in sends:
        send.wait()


def last_pass(own, words, scored, lse, near, direct, owned, tile, chunk):
    depth = words.shape[1]
    rows = scored.shape[1]
    count = len(near)
    return pl.pallas_call(
        functools.partial(last_kernel, count, tile, chunk),
        in_specs=[SMEM, HBM, VMEM, VMEM] + [HBM] * (2 * count),
        out_specs=HBM,
        scratch_shapes=[
            pltpu.VMEM((2 * rows, depth), bf16),
            pltpu.VMEM((owned, depth), bf16),
            pltpu.VMEM((owned, 2 * rows), bf16),
            pltpu.VMEM((owned, depth), f32),
            pltpu.SemaphoreType.DMA((2 * count + 1,)),
            pltpu.SemaphoreType.DMA((owned // tile,)),
        ],
        out_shape=jax.ShapeDtypeStruct((owned, depth), f32),
        name="last_pass",
        compiler_params=pltpu.CompilerParams(vmem_limit_bytes=50 * 2**20),
    )(own, words, scored, lse, *near, *direct)


def to_other(value, axis, flip):
    return lax.ppermute(value, axis, [(i, i ^ flip) for i in range(lax.axis_size(axis))])


def to_column(value, step):
    n = lax.axis_size("dp")
    table = []
    for book in range(2):
        for core in range(2):
            hop = step ^ 1 if core == 0 else step ^ 1 ^ (n // 2 - 1)
            for d in range(n):
                here = (book * 2 + core) * n + d
                there = ((1 - book) * 2 + core) * n + (d ^ (2 * hop))
                table.append((here, there))
    return lax.ppermute(value, ("pair", "code", "dp"), table)


def hbm_named(call, *args):
    return pltpu.with_memory_space_constraint(call(*args), pltpu.HBM)


def step(samples, codebooks):
    words = pltpu.with_memory_space_constraint(codebooks[0], pltpu.HBM)
    rows, _ = samples.shape
    half = rows // 2
    n = lax.axis_size("dp")
    owned = words.shape[0] // n
    core = lax.axis_index("code").reshape(1)
    own = lax.axis_index("dp").reshape(1)
    mine, other = first_pass(
        core, pltpu.with_memory_space_constraint(samples, pltpu.HBM), words, 1024
    )
    theirs = to_other(other, "code", 1)
    residual = join(core, samples, mine, theirs)

    direct = [hbm_named(to_column, residual, i) for i in range(n // 2)]
    swapped = [hbm_named(to_other, direct[i], "code", 1) for i in range(n // 2)]
    near = [hbm_named(to_other, direct[i], "dp", 1) for i in range(n // 2)]
    near_swapped = [hbm_named(to_other, near[i], "code", 1) for i in range(n // 2)]

    lse = stats_pass(direct[0], swapped[0], words, 1024)
    far = to_other(lse, "code", 1)
    far = jnp.concatenate([far[:, half:], far[:, :half]], axis=1)
    lse = jnp.logaddexp(lse, far)
    flip = 1
    while flip < n:
        lse = jnp.concatenate([lse, to_other(lse, "dp", flip)], axis=0)
        flip *= 2
    lse = jnp.stack([lse[0::2].reshape(-1), lse[1::2].reshape(-1)])

    direct = [v for pair in zip(direct, swapped) for v in pair]
    near = [v for pair in zip(near, near_swapped) for v in pair]
    scored = score_pass(own, words, direct, owned)
    updated = last_pass(
        own, words, scored, lse, near, direct, owned, max(owned // 4, 128), 2 * rows
    )
    return updated[None]


def solution(mesh):
    in_specs = (P("dp", None), P("pair", "code", None))
    out_specs = P("pair", ("code", "dp"), None)
    return jax.shard_map(step, mesh=mesh, in_specs=in_specs, out_specs=out_specs, check_vma=False)
```

time: 656 us -> 83.4 us (0.13)
  waiting for transfers between devices: 490 us -> 20.4 us
  matrix products: 50.6 us -> 0 us
  blocking collectives: 50 us -> 0 us
  other arithmetic: 44.3 us -> 1.13 us
  Pallas kernels: 0 us -> 37.9 us
  starting transfers between devices: 2.87 us -> 22.5 us
  between operations: 14.8 us -> 0.15 us
    reduce_scatter x1 -> x0, waiting for transfers between devices: 480 us -> none  [shards(): lax.psum_scatter(partial_value, 'dp', scatter_dimension=0, tiled=True)]
    dot_general x4 -> x0, matrix products: 50.6 us -> none  [the longest x2 28.2 us: scores_of(): lax.dot_general(block, words, (((1,), (1,)), ((), ())), preferred_element...]
    unnamed x2 -> x0, blocking collectives: 42.6 us -> none
    pallas_call x0 -> x4, Pallas kernels: none -> 37.9 us  [the longest x1 14.1 us: first_pass(): pl.pallas_call(functools.partial(first_kernel, tile), in_specs=[SMEM, HBM...]
    ppermute x1 -> x21, starting transfers between devices: 2.87 us -> 22.5 us  [the longest x17 12 us: to_other(): lax.ppermute(value, axis, [(i, i ^ flip) for i in range(lax.axis_size(axi...]
    convert_element_type x3 -> x1, other arithmetic: 18.9 us -> 0.17 us  [join(): return (own.astype(f32) - rebuilt.astype(bf16).astype(f32)).astype(bf16)]
    reduce_sum x4 -> x0, other arithmetic: 18.5 us -> none  [the longest x1 7.23 us: shards(): sq_norms = jnp.sum(words32 * words32, axis=-1)]
    ppermute x1 -> x21, waiting for transfers between devices: 9.45 us -> 20.4 us  [the longest x17 14.5 us: to_other(): lax.ppermute(value, axis, [(i, i ^ flip) for i in range(lax.axis_size(axi...]
  transfers between devices with their start and end apart: 2 -> 21, of which waited for: 2 -> 8; matrix products, arithmetic and copies ran while one was open for 3% -> 1% of each run, Pallas kernels for 0% -> 17%
where the time goes in v2:
time: 83.4 us; the launch traced here: 83.3 us
  Pallas kernels  37.9 us (45%)
  starting transfers between devices  22.5 us (27%)
  waiting for transfers between devices  20.4 us (24%)
  other arithmetic  1.13 us (1%)
  local copies, waits for them, and re-layouts  1.12 us (1%)
    ppermute x17, waiting for transfers between devices, to_other(): lax.ppermute(value, axis, [(i, i ^ flip) for i in range(lax.axis_size(axi...  14.5 us
    pallas_call x1, Pallas kernels, first_pass(): pl.pallas_call(functools.partial(first_kernel, tile), in_specs=[SMEM, HBM...  14.1 us
    ppermute x17, starting transfers between devices, to_other(): lax.ppermute(value, axis, [(i, i ^ flip) for i in range(lax.axis_size(axi...  12 us
    ppermute x4, starting transfers between devices, to_column(): return lax.ppermute(value, ('pair', 'code', 'dp'), table)  10.6 us
    pallas_call x1, Pallas kernels, stats_pass(): pl.pallas_call(functools.partial(stats_kernel, tile), in_specs=[HBM, HBM,...  10.3 us
    pallas_call x1, Pallas kernels, last_pass(): pl.pallas_call(functools.partial(last_kernel, count, tile, chunk), in_spe...  9.48 us
    ppermute x4, waiting for transfers between devices, to_column(): return lax.ppermute(value, ('pair', 'code', 'dp'), table)  5.94 us
    pallas_call x1, Pallas kernels, score_pass(): pl.pallas_call(functools.partial(score_kernel, len(pieces)), in_specs=[SM...  4 us
  transfers between devices with their start and end apart: 21, of which 8 were waited for; matrix products, arithmetic and copies ran while one was open for 1% of the time, Pallas kernels for 17%

profile of v2, /device:TPU:0, one launch (start us, length us, event | category | flops | bytes accessed | tf_op | source)
XLA Modules:
  0.0 83.3 jit_solution(15143929545163777852)
XLA Ops:
  0.0 14.1 %first_pass.1 = (f32[96,1280]{1,0:T(8,128)S(1)}, f32[96,1280]{1,0:T(8,128)S(1)}) custom-call(s32[1]{0:T(128)} %bitcast.2.core, bf16[192,1024]{1,0:T(8,128)(2,1)} %s_hbm.1, bf16[8192,1024]{1,0:T(8,128)(2,1)} %bitcast.4), custom_call_target="tpu_custom_call" | custom-call | tf_op jit(solution)/shard_map/first_pass/pallas_call | solution.py:100
  14.1 0.6 collective-permute-start
  14.7 1.5 %collective-permute-done = f32[96,1280]{1,0:T(8,128)S(1)} collective-permute-done((f32[96,1280]{1,0:T(8,128)S(1)}, f32[96,1280]{1,0:T(8,128)S(1)}, u32[]{:S(2)}, u32[]{:S(2)}) %collective-permute-start) | collective-permute-done | bytes 491552 | tf_op jit(solution)/shard_map/ppermute | solution.py:298
  16.2 0.2 fusion.8
  16.4 0.2 subtract_convert_fusion
  16.6 3.9 %collective-permute-start.1 = (bf16[96,1024]{1,0:T(8,128)(2,1)S(1)}, bf16[96,1024]{1,0:T(8,128)(2,1)S(1)}, u32[]{:S(2)}, u32[]{:S(2)}) collective-permute-start(bf16[96,1024]{1,0:T(8,128)(2,1)S(1)} %subtract_convert_fusion), channel_id=1, source_target_pairs={{0,18},{1,19},{2,16},{3,17},{4,22},{5,23},{6,20},{7,21},{8,28},{9,... | collective-permute-start | bytes 589832 | tf_op jit(solution)/shard_map/ppermute | solution.py:311
  20.5 5.3 %collective-permute-done.1.refs_0_.a_hbm.refs_8_ = bf16[96,1024]{1,0:T(8,128)(2,1)S(1)} collective-permute-done((bf16[96,1024]{1,0:T(8,128)(2,1)S(1)}, bf16[96,1024]{1,0:T(8,128)(2,1)S(1)}, u32[]{:S(2)}, u32[]{:S(2)}) %collective-permute-start.1) | collective-permute-done | bytes 196640 | tf_op jit(solution)/shard_map/ppermute | solution.py:311
  25.8 0.6 collective-permute-start.2
  26.4 3.6 %collective-permute-start.7 = (bf16[96,1024]{1,0:T(8,128)(2,1)S(1)}, bf16[96,1024]{1,0:T(8,128)(2,1)S(1)}, u32[]{:S(2)}, u32[]{:S(2)}) collective-permute-start(bf16[96,1024]{1,0:T(8,128)(2,1)S(1)} %subtract_convert_fusion), channel_id=1, source_target_pairs={{0,20},{1,21},{2,22},{3,23},{4,16},{5,17},{6,18},{7,19},{8,26},{9,... | collective-permute-start | bytes 589832 | tf_op jit(solution)/shard_map/ppermute | solution.py:311
  30.0 0.7 copy-done.1
  30.7 10.3 %stats_pass.1 = f32[1,192]{1,0:T(1,128)} custom-call(bf16[96,1024]{1,0:T(8,128)(2,1)} %copy-done, bf16[96,1024]{1,0:T(8,128)(2,1)} %copy-done.1, bf16[8192,1024]{1,0:T(8,128)(2,1)} %bitcast.5), custom_call_target="tpu_custom_call" | custom-call | flops 3221225472 | bytes 16777216 | tf_op jit(solution)/shard_map/stats_pass/pallas_call | solution.py:173
  41.1 2.6 %collective-permute-start.5 = (bf16[96,1024]{1,0:T(8,128)(2,1)S(1)}, bf16[96,1024]{1,0:T(8,128)(2,1)S(1)}, u32[]{:S(2)}, u32[]{:S(2)}) collective-permute-start(bf16[96,1024]{1,0:T(8,128)(2,1)S(1)} %subtract_convert_fusion), channel_id=1, source_target_pairs={{0,22},{1,23},{2,20},{3,21},{4,18},{5,19},{6,16},{7,17},{8,24},{9,... | collective-permute-start | bytes 589832 | tf_op jit(solution)/shard_map/ppermute | solution.py:311
  43.7 0.5 collective-permute-start.3
  44.2 1.5 %collective-permute-start.19 = (bf16[96,1024]{1,0:T(8,128)(2,1)S(1)}, bf16[96,1024]{1,0:T(8,128)(2,1)}, u32[]{:S(2)}, u32[]{:S(2)}) collective-permute-start(bf16[96,1024]{1,0:T(8,128)(2,1)S(1)} %collective-permute-done.7.refs_6_.refs_14_), channel_id=1, source_target_pairs={{0,1},{1,0},{2,3},{3,2},{4,5},{5,4},{6,7},{7,6},{8,9},{9,8},{10,11... | collective-permute-start | bytes 589832 | tf_op jit(solution)/shard_map/ppermute | solution.py:298
  45.8 0.8 compare_select_fusion
  46.6 0.7 collective-permute-start.10
  47.3 3.6 %collective-permute-done.10 = f32[1,192]{1,0:T(1,128)S(1)} collective-permute-done((f32[1,192]{1,0:T(1,128)S(1)}, f32[1,192]{1,0:T(1,128)S(1)}, u32[]{:S(2)}, u32[]{:S(2)}) %collective-permute-start.10) | collective-permute-done | bytes 800 | tf_op jit(solution)/shard_map/ppermute | solution.py:298
  51.0 0.5 collective-permute-start.11
  51.5 0.1 collective-permute-done.5.refs_4_.refs_12_
  51.6 1.5 %collective-permute-start.17 = (bf16[96,1024]{1,0:T(8,128)(2,1)S(1)}, bf16[96,1024]{1,0:T(8,128)(2,1)}, u32[]{:S(2)}, u32[]{:S(2)}) collective-permute-start(bf16[96,1024]{1,0:T(8,128)(2,1)S(1)} %collective-permute-done.5.refs_4_.refs_12_), channel_id=1, source_target_pairs={{0,1},{1,0},{2,3},{3,2},{4,5},{5,4},{6,7},{7,6},{8,9},{9,8},{10,11... | collective-permute-start | bytes 589832 | tf_op jit(solution)/shard_map/ppermute | solution.py:298
  53.1 0.5 collective-permute-done.3.refs_2_.refs_10_
  53.6 1.6 %collective-permute-start.15 = (bf16[96,1024]{1,0:T(8,128)(2,1)S(1)}, bf16[96,1024]{1,0:T(8,128)(2,1)}, u32[]{:S(2)}, u32[]{:S(2)}) collective-permute-start(bf16[96,1024]{1,0:T(8,128)(2,1)S(1)} %collective-permute-done.3.refs_2_.refs_10_), channel_id=1, source_target_pairs={{0,1},{1,0},{2,3},{3,2},{4,5},{5,4},{6,7},{7,6},{8,9},{9,8},{10,11... | collective-permute-start | bytes 589832 | tf_op jit(solution)/shard_map/ppermute | solution.py:298
  55.1 0.5 collective-permute-start.13
  55.7 0.1 copy-done.6
  55.8 0.2 collective-permute-start.4
  56.0 2.0 %collective-permute-done.17.refs_4_ = bf16[96,1024]{1,0:T(8,128)(2,1)} collective-permute-done((bf16[96,1024]{1,0:T(8,128)(2,1)S(1)}, bf16[96,1024]{1,0:T(8,128)(2,1)}, u32[]{:S(2)}, u32[]{:S(2)}) %collective-permute-start.17) | collective-permute-done | bytes 196640 | tf_op jit(solution)/shard_map/ppermute | solution.py:298
  58.0 0.5 collective-permute-start.18
  58.5 3.7 %collective-permute-done.15.refs_2_ = bf16[96,1024]{1,0:T(8,128)(2,1)} collective-permute-done((bf16[96,1024]{1,0:T(8,128)(2,1)S(1)}, bf16[96,1024]{1,0:T(8,128)(2,1)}, u32[]{:S(2)}, u32[]{:S(2)}) %collective-permute-start.15) | collective-permute-done | bytes 196640 | tf_op jit(solution)/shard_map/ppermute | solution.py:298
  62.2 3.6 %collective-permute-done.13.refs_0_ = bf16[96,1024]{1,0:T(8,128)(2,1)} collective-permute-done((bf16[96,1024]{1,0:T(8,128)(2,1)}, bf16[96,1024]{1,0:T(8,128)(2,1)}, u32[]{:S(2)}, u32[]{:S(2)}) %collective-permute-start.13) | collective-permute-done | bytes 196640 | tf_op jit(solution)/shard_map/ppermute | solution.py:298
  65.8 3.6 %collective-permute-start.12 = (f32[4,192]{1,0:T(4,128)S(1)}, f32[4,192]{1,0:T(4,128)S(1)}, u32[]{:S(2)}, u32[]{:S(2)}) collective-permute-start(f32[4,192]{1,0:T(4,128)S(1)} %pad_maximum_fusion.2), channel_id=1, source_target_pairs={{0,4},{1,5},{2,6},{3,7},{4,0},{5,1},{6,2},{7,3},{8,12},{9,13},{10,... | collective-permute-start | bytes 9224 | tf_op jit(solution)/shard_map/ppermute | solution.py:298
  69.5 4.0 %score_pass.1.la_ref = f32[1024,768]{1,0:T(8,128)S(1)} custom-call(s32[1]{0:T(128)} %bitcast.own, bf16[8192,1024]{1,0:T(8,128)(2,1)} %bitcast.6, bf16[96,1024]{1,0:T(8,128)(2,1)} %copy-done, bf16[96,1024]{1,0:T(8,128)(2,1)} %copy-done.1, bf16[96,1024]{1,0:T(8,128)(2,1)} %copy-done.5, bf16[96,1024]{1,0:T(8,128)(2,1)} %copy-done.8, ...), custom_call_target="tpu_custom_call" | custom-call | flops 1610612736 | bytes 1572864 | tf_op jit(solution)/shard_map/score_pass/pallas_call | solution.py:221
  73.8 9.5 %last_pass.1 = f32[1024,1024]{1,0:T(8,128)} custom-call(s32[1]{0:T(128)} %bitcast.own, bf16[8192,1024]{1,0:T(8,128)(2,1)} %bitcast.7, f32[1024,768]{1,0:T(8,128)S(1)} %score_pass.1.la_ref, f32[2,768]{1,0:T(2,128)S(1)} %pad_maximum_fusion.1.lse_ref, bf16[96,1024]{1,0:T(8,128)(2,1)} %collective-permute-done.13.refs_0_, ...), custom_call_target="tpu_custom_call" | custom-call | tf_op jit(solution)/shard_map/last_pass/pallas_call | solution.py:279
  (44 shorter events, 0.5 us)
Async XLA Ops:
  0.0 16.4 %copy-start.2 = (bf16[192,1024]{1,0:T(8,128)(2,1)S(1)}, bf16[192,1024]{1,0:T(8,128)(2,1)}, u32[]{:S(2)}) copy-start(bf16[192,1024]{1,0:T(8,128)(2,1)} %s_hbm.1) | copy-start | bytes 1179652
  14.1 2.1 %collective-permute-start = (f32[96,1280]{1,0:T(8,128)S(1)}, f32[96,1280]{1,0:T(8,128)S(1)}, u32[]{:S(2)}, u32[]{:S(2)}) collective-permute-start(f32[96,1280]{1,0:T(8,128)S(1)} %get-tuple-element.8), channel_id=1, source_target_pairs={{0,8},{8,0},{1,9},{9,1},{2,10},{10,2},{3,11},{11,3},{4,12},{12,4},... | collective-permute-start | bytes 1474568 | tf_op jit(solution)/shard_map/ppermute | solution.py:298
  16.6 9.2 %collective-permute-start.1 = (bf16[96,1024]{1,0:T(8,128)(2,1)S(1)}, bf16[96,1024]{1,0:T(8,128)(2,1)S(1)}, u32[]{:S(2)}, u32[]{:S(2)}) collective-permute-start(bf16[96,1024]{1,0:T(8,128)(2,1)S(1)} %subtract_convert_fusion), channel_id=1, source_target_pairs={{0,18},{1,19},{2,16},{3,17},{4,22},{5,23},{6,20},{7,21},{8,28},{9,... | collective-permute-start | bytes 589832 | tf_op jit(solution)/shard_map/ppermute | solution.py:311
  25.8 4.2 %copy-start = (bf16[96,1024]{1,0:T(8,128)(2,1)}, bf16[96,1024]{1,0:T(8,128)(2,1)S(1)}, u32[]{:S(2)}) copy-start(bf16[96,1024]{1,0:T(8,128)(2,1)S(1)} %collective-permute-done.1.refs_0_.a_hbm.refs_8_) | copy-start | bytes 589828
  25.8 4.2 %collective-permute-start.2 = (bf16[96,1024]{1,0:T(8,128)(2,1)S(1)}, bf16[96,1024]{1,0:T(8,128)(2,1)S(1)}, u32[]{:S(2)}, u32[]{:S(2)}) collective-permute-start(bf16[96,1024]{1,0:T(8,128)(2,1)S(1)} %collective-permute-done.1.refs_0_.a_hbm.refs_8_), channel_id=1, source_target_pairs={{0,8},{8,0},{1,9},{9,1},{2,10},{10,2},{3,11},{11,3},{4,12},{12,4},... | collective-permute-start | bytes 589832 | tf_op jit(solution)/shard_map/ppermute | solution.py:298
  26.4 17.8 %collective-permute-start.7 = (bf16[96,1024]{1,0:T(8,128)(2,1)S(1)}, bf16[96,1024]{1,0:T(8,128)(2,1)S(1)}, u32[]{:S(2)}, u32[]{:S(2)}) collective-permute-start(bf16[96,1024]{1,0:T(8,128)(2,1)S(1)} %subtract_convert_fusion), channel_id=1, source_target_pairs={{0,20},{1,21},{2,22},{3,23},{4,16},{5,17},{6,18},{7,19},{8,26},{9,... | collective-permute-start | bytes 589832 | tf_op jit(solution)/shard_map/ppermute | solution.py:311
  30.0 0.7 copy-start.1
  41.0 4.7 %collective-permute-start.9 = (f32[1,192]{1,0:T(1,128)}, f32[1,192]{1,0:T(1,128)S(1)}, u32[]{:S(2)}, u32[]{:S(2)}) collective-permute-start(f32[1,192]{1,0:T(1,128)} %stats_pass.1), channel_id=1, source_target_pairs={{0,8},{8,0},{1,9},{9,1},{2,10},{10,2},{3,11},{11,3},{4,12},{12,4},... | collective-permute-start | bytes 2312 | tf_op jit(solution)/shard_map/ppermute | solution.py:298
  41.1 10.5 %collective-permute-start.5 = (bf16[96,1024]{1,0:T(8,128)(2,1)S(1)}, bf16[96,1024]{1,0:T(8,128)(2,1)S(1)}, u32[]{:S(2)}, u32[]{:S(2)}) collective-permute-start(bf16[96,1024]{1,0:T(8,128)(2,1)S(1)} %subtract_convert_fusion), channel_id=1, source_target_pairs={{0,22},{1,23},{2,20},{3,21},{4,18},{5,19},{6,16},{7,17},{8,24},{9,... | collective-permute-start | bytes 589832 | tf_op jit(solution)/shard_map/ppermute | solution.py:311
  43.7 9.9 %collective-permute-start.3 = (bf16[96,1024]{1,0:T(8,128)(2,1)S(1)}, bf16[96,1024]{1,0:T(8,128)(2,1)S(1)}, u32[]{:S(2)}, u32[]{:S(2)}) collective-permute-start(bf16[96,1024]{1,0:T(8,128)(2,1)S(1)} %subtract_convert_fusion), channel_id=1, source_target_pairs={{0,16},{1,17},{2,18},{3,19},{4,20},{5,21},{6,22},{7,23},{8,30},{9,... | collective-permute-start | bytes 589832 | tf_op jit(solution)/shard_map/ppermute | solution.py:311
  44.2 1.5 %copy-start.3 = (bf16[96,1024]{1,0:T(8,128)(2,1)}, bf16[96,1024]{1,0:T(8,128)(2,1)S(1)}, u32[]{:S(2)}) copy-start(bf16[96,1024]{1,0:T(8,128)(2,1)S(1)} %collective-permute-done.7.refs_6_.refs_14_) | copy-start | bytes 589828
  44.2 9.3 %collective-permute-start.19 = (bf16[96,1024]{1,0:T(8,128)(2,1)S(1)}, bf16[96,1024]{1,0:T(8,128)(2,1)}, u32[]{:S(2)}, u32[]{:S(2)}) collective-permute-start(bf16[96,1024]{1,0:T(8,128)(2,1)S(1)} %collective-permute-done.7.refs_6_.refs_14_), channel_id=1, source_target_pairs={{0,1},{1,0},{2,3},{3,2},{4,5},{5,4},{6,7},{7,6},{8,9},{9,8},{10,11... | collective-permute-start | bytes 589832 | tf_op jit(solution)/shard_map/ppermute | solution.py:298
  45.7 9.4 %collective-permute-start.8 = (bf16[96,1024]{1,0:T(8,128)(2,1)S(1)}, bf16[96,1024]{1,0:T(8,128)(2,1)S(1)}, u32[]{:S(2)}, u32[]{:S(2)}) collective-permute-start(bf16[96,1024]{1,0:T(8,128)(2,1)S(1)} %collective-permute-done.7.refs_6_.refs_14_), channel_id=1, source_target_pairs={{0,8},{8,0},{1,9},{9,1},{2,10},{10,2},{3,11},{11,3},{4,12},{12,4},... | collective-permute-start | bytes 589832 | tf_op jit(solution)/shard_map/ppermute | solution.py:298
  46.6 4.4 %collective-permute-start.10 = (f32[1,192]{1,0:T(1,128)S(1)}, f32[1,192]{1,0:T(1,128)S(1)}, u32[]{:S(2)}, u32[]{:S(2)}) collective-permute-start(f32[1,192]{1,0:T(1,128)S(1)} %compare_select_fusion), channel_id=1, source_target_pairs={{0,1},{1,0},{2,3},{3,2},{4,5},{5,4},{6,7},{7,6},{8,9},{9,8},{10,11... | collective-permute-start | bytes 2312 | tf_op jit(solution)/shard_map/ppermute | solution.py:298
  51.0 4.8 %collective-permute-start.11 = (f32[2,192]{1,0:T(2,128)S(1)}, f32[2,192]{1,0:T(2,128)S(1)}, u32[]{:S(2)}, u32[]{:S(2)}) collective-permute-start(f32[2,192]{1,0:T(2,128)S(1)} %pad_maximum_fusion.3), channel_id=1, source_target_pairs={{0,2},{1,3},{2,0},{3,1},{4,6},{5,7},{6,4},{7,5},{8,10},{9,11},{10,... | collective-permute-start | bytes 4616 | tf_op jit(solution)/shard_map/ppermute | solution.py:298
  51.6 17.9 %copy-start.4 = (bf16[96,1024]{1,0:T(8,128)(2,1)}, bf16[96,1024]{1,0:T(8,128)(2,1)S(1)}, u32[]{:S(2)}) copy-start(bf16[96,1024]{1,0:T(8,128)(2,1)S(1)} %collective-permute-done.5.refs_4_.refs_12_) | copy-start | bytes 589828
  51.6 6.5 %collective-permute-start.17 = (bf16[96,1024]{1,0:T(8,128)(2,1)S(1)}, bf16[96,1024]{1,0:T(8,128)(2,1)}, u32[]{:S(2)}, u32[]{:S(2)}) collective-permute-start(bf16[96,1024]{1,0:T(8,128)(2,1)S(1)} %collective-permute-done.5.refs_4_.refs_12_), channel_id=1, source_target_pairs={{0,1},{1,0},{2,3},{3,2},{4,5},{5,4},{6,7},{7,6},{8,9},{9,8},{10,11... | collective-permute-start | bytes 589832 | tf_op jit(solution)/shard_map/ppermute | solution.py:298
  53.6 15.9 %copy-start.5 = (bf16[96,1024]{1,0:T(8,128)(2,1)}, bf16[96,1024]{1,0:T(8,128)(2,1)S(1)}, u32[]{:S(2)}) copy-start(bf16[96,1024]{1,0:T(8,128)(2,1)S(1)} %collective-permute-done.3.refs_2_.refs_10_) | copy-start | bytes 589828
  53.6 4.5 %collective-permute-start.6 = (bf16[96,1024]{1,0:T(8,128)(2,1)S(1)}, bf16[96,1024]{1,0:T(8,128)(2,1)S(1)}, u32[]{:S(2)}, u32[]{:S(2)}) collective-permute-start(bf16[96,1024]{1,0:T(8,128)(2,1)S(1)} %collective-permute-done.5.refs_4_.refs_12_), channel_id=1, source_target_pairs={{0,8},{8,0},{1,9},{9,1},{2,10},{10,2},{3,11},{11,3},{4,12},{12,4},... | collective-permute-start | bytes 589832 | tf_op jit(solution)/shard_map/ppermute | solution.py:298
  53.6 8.7 %collective-permute-start.15 = (bf16[96,1024]{1,0:T(8,128)(2,1)S(1)}, bf16[96,1024]{1,0:T(8,128)(2,1)}, u32[]{:S(2)}, u32[]{:S(2)}) collective-permute-start(bf16[96,1024]{1,0:T(8,128)(2,1)S(1)} %collective-permute-done.3.refs_2_.refs_10_), channel_id=1, source_target_pairs={{0,1},{1,0},{2,3},{3,2},{4,5},{5,4},{6,7},{7,6},{8,9},{9,8},{10,11... | collective-permute-start | bytes 589832 | tf_op jit(solution)/shard_map/ppermute | solution.py:298
  55.1 0.7 copy-start.6
  55.1 10.7 %collective-permute-start.13 = (bf16[96,1024]{1,0:T(8,128)(2,1)}, bf16[96,1024]{1,0:T(8,128)(2,1)}, u32[]{:S(2)}, u32[]{:S(2)}) collective-permute-start(bf16[96,1024]{1,0:T(8,128)(2,1)} %copy-done), channel_id=1, source_target_pairs={{0,1},{1,0},{2,3},{3,2},{4,5},{5,4},{6,7},{7,6},{8,9},{9,8},{10,11... | collective-permute-start | bytes 589832 | tf_op jit(solution)/shard_map/ppermute | solution.py:298
  55.8 10.0 %collective-permute-start.4 = (bf16[96,1024]{1,0:T(8,128)(2,1)S(1)}, bf16[96,1024]{1,0:T(8,128)(2,1)S(1)}, u32[]{:S(2)}, u32[]{:S(2)}) collective-permute-start(bf16[96,1024]{1,0:T(8,128)(2,1)S(1)} %collective-permute-done.3.refs_2_.refs_10_), channel_id=1, source_target_pairs={{0,8},{8,0},{1,9},{9,1},{2,10},{10,2},{3,11},{11,3},{4,12},{12,4},... | collective-permute-start | bytes 589832 | tf_op jit(solution)/shard_map/ppermute | solution.py:298
  58.0 15.7 %collective-permute-start.20 = (bf16[96,1024]{1,0:T(8,128)(2,1)}, bf16[96,1024]{1,0:T(8,128)(2,1)}, u32[]{:S(2)}, u32[]{:S(2)}) collective-permute-start(bf16[96,1024]{1,0:T(8,128)(2,1)} %collective-permute-done.19.refs_6_), channel_id=1, source_target_pairs={{0,8},{8,0},{1,9},{9,1},{2,10},{10,2},{3,11},{11,3},{4,12},{12,4},... | collective-permute-start | bytes 589832 | tf_op jit(solution)/shard_map/ppermute | solution.py:298
  58.0 11.4 %copy-start.7 = (bf16[96,1024]{1,0:T(8,128)(2,1)}, bf16[96,1024]{1,0:T(8,128)(2,1)S(1)}, u32[]{:S(2)}) copy-start(bf16[96,1024]{1,0:T(8,128)(2,1)S(1)} %collective-permute-done.6.refs_5_.refs_13_) | copy-start | bytes 589828
  58.0 15.7 %collective-permute-start.18 = (bf16[96,1024]{1,0:T(8,128)(2,1)}, bf16[96,1024]{1,0:T(8,128)(2,1)}, u32[]{:S(2)}, u32[]{:S(2)}) collective-permute-start(bf16[96,1024]{1,0:T(8,128)(2,1)} %collective-permute-done.17.refs_4_), channel_id=1, source_target_pairs={{0,8},{8,0},{1,9},{9,1},{2,10},{10,2},{3,11},{11,3},{4,12},{12,4},... | collective-permute-start | bytes 589832 | tf_op jit(solution)/shard_map/ppermute | solution.py:298
  62.2 11.5 %collective-permute-start.16 = (bf16[96,1024]{1,0:T(8,128)(2,1)}, bf16[96,1024]{1,0:T(8,128)(2,1)}, u32[]{:S(2)}, u32[]{:S(2)}) collective-permute-start(bf16[96,1024]{1,0:T(8,128)(2,1)} %collective-permute-done.15.refs_2_), channel_id=1, source_target_pairs={{0,8},{8,0},{1,9},{9,1},{2,10},{10,2},{3,11},{11,3},{4,12},{12,4},... | collective-permute-start | bytes 589832 | tf_op jit(solution)/shard_map/ppermute | solution.py:298
  65.8 8.0 %collective-permute-start.14 = (bf16[96,1024]{1,0:T(8,128)(2,1)}, bf16[96,1024]{1,0:T(8,128)(2,1)}, u32[]{:S(2)}, u32[]{:S(2)}) collective-permute-start(bf16[96,1024]{1,0:T(8,128)(2,1)} %collective-permute-done.13.refs_0_), channel_id=1, source_target_pairs={{0,8},{8,0},{1,9},{9,1},{2,10},{10,2},{3,11},{11,3},{4,12},{12,4},... | collective-permute-start | bytes 589832 | tf_op jit(solution)/shard_map/ppermute | solution.py:298
  65.8 3.6 %copy-start.8 = (bf16[96,1024]{1,0:T(8,128)(2,1)}, bf16[96,1024]{1,0:T(8,128)(2,1)S(1)}, u32[]{:S(2)}) copy-start(bf16[96,1024]{1,0:T(8,128)(2,1)S(1)} %collective-permute-done.4.refs_3_.refs_11_) | copy-start | bytes 589828
  65.8 7.7 %collective-permute-start.12 = (f32[4,192]{1,0:T(4,128)S(1)}, f32[4,192]{1,0:T(4,128)S(1)}, u32[]{:S(2)}, u32[]{:S(2)}) collective-permute-start(f32[4,192]{1,0:T(4,128)S(1)} %pad_maximum_fusion.2), channel_id=1, source_target_pairs={{0,4},{1,5},{2,6},{3,7},{4,0},{5,1},{6,2},{7,3},{8,12},{9,13},{10,... | collective-permute-start | bytes 9224 | tf_op jit(solution)/shard_map/ppermute | solution.py:298

commit v3 on v2

--- a/solution.py
+++ b/solution.py
@@ -19,6 +19,7 @@
 VMEM = pl.BlockSpec(memory_space=pltpu.VMEM)
 SMEM = pl.BlockSpec(memory_space=pltpu.SMEM)
 HBM = pl.BlockSpec(memory_space=pltpu.HBM)
+ANY = pl.BlockSpec(memory_space=pl.ANY)
 
 
 def square_sums(words):
@@ -131,17 +132,30 @@
     return (own.astype(f32) - rebuilt.astype(bf16).astype(f32)).astype(bf16)
 
 
-def stats_kernel(tile, a_hbm, b_hbm, w_hbm, lse, held, top, total, twice, sems, row_sems):
+def early_kernel(held, out):
+    out[...] = held[: out.shape[0], : out.shape[1]]
+
+
+def early_pass(words):
+    return pl.pallas_call(
+        early_kernel,
+        in_specs=[VMEM],
+        out_specs=VMEM,
+        out_shape=jax.ShapeDtypeStruct((2 * SUBLANES, LANES), words.dtype),
+        name="early_pass",
+        compiler_params=pltpu.CompilerParams(vmem_limit_bytes=2**20),
+    )(words)
+
+
+def stats_kernel(tile, core, a_hbm, b_hbm, held, early, lse, top, total, twice, row_sems):
     half = a_hbm.shape[0]
     steps = held.shape[0] // tile
     fetches = [
-        pltpu.make_async_copy(source, twice.at[pl.ds(i * half, half)], row_sems.at[i])
-        for i, source in enumerate((a_hbm, b_hbm))
+        pltpu.make_async_copy(source, twice.at[span(place, half)], row_sems.at[i])
+        for i, (source, place) in enumerate(((a_hbm, core[0]), (b_hbm, 1 - core[0])))
     ]
     for fetch in fetches:
         fetch.start()
-    for t in range(min(AHEAD, steps)):
-        tile_copy(w_hbm, held, sems, tile, t).start()
     for fetch in fetches:
         fetch.wait()
     twice[...] = twice[...] * 2
@@ -150,11 +164,6 @@
 
     @pl.loop(0, steps)
     def _(t):
-        @pl.when(t + AHEAD < steps)
-        def _():
-            tile_copy(w_hbm, held, sems, tile, t + AHEAD).start()
-
-        tile_copy(w_hbm, held, sems, tile, t).wait()
         words = held[span(t, tile)]
         score = lax.dot_general(words, twice[...], NT, preferred_element_type=f32)
         score = (score - square_sums(words)).reshape(tile // SUBLANES, SUBLANES, 2 * half)
@@ -167,44 +176,42 @@
     lse[...] = best + jnp.log(jnp.sum(total[...] * jnp.exp(top[...] - best), axis=0, keepdims=True))
 
 
-def stats_pass(first, second, words, tile):
+def stats_pass(core, first, second, words, early, tile):
     half, depth = first.shape
     count = words.shape[0]
     return pl.pallas_call(
         functools.partial(stats_kernel, tile),
-        in_specs=[HBM, HBM, HBM],
+        in_specs=[SMEM, ANY, ANY, VMEM, ANY],
         out_specs=VMEM,
         out_shape=jax.ShapeDtypeStruct((1, 2 * half), f32),
         scratch_shapes=[
-            pltpu.VMEM((count, depth), bf16),
             pltpu.VMEM((SUBLANES, 2 * half), f32),
             pltpu.VMEM((SUBLANES, 2 * half), f32),
             pltpu.VMEM((2 * half, depth), bf16),
-            pltpu.SemaphoreType.DMA((count // tile,)),
             pltpu.SemaphoreType.DMA((2,)),
         ],
         name="stats_pass",
         cost_estimate=pl.CostEstimate(
             flops=4 * half * count * depth, bytes_accessed=2 * count * depth, transcendentals=0
         ),
-        compiler_params=pltpu.CompilerParams(vmem_limit_bytes=60 * 2**20),
-    )(first, second, words)
-
-
-def row_fetches(pieces, block, sems, first):
-    fetches, at = [], 0
+        compiler_params=pltpu.CompilerParams(vmem_limit_bytes=24 * 2**20),
+    )(core, first, second, words, early)
+
+
+def row_fetches(core, pieces, block, sems, first):
+    fetches = []
     for i, piece in enumerate(pieces):
-        rows = piece.shape[0]
-        fetches.append(pltpu.make_async_copy(piece, block.at[pl.ds(at, rows)], sems.at[first + i]))
-        at += rows
+        half = piece.shape[0]
+        place = i - i % 2 + (core[0] if i % 2 == 0 else 1 - core[0])
+        fetches.append(pltpu.make_async_copy(piece, block.at[span(place, half)], sems.at[first + i]))
     return fetches
 
 
-def score_kernel(count, own, w_hbm, *refs):
+def score_kernel(count, core, own, w_hbm, *refs):
     pieces, (logits, block, words, sems) = refs[:count], refs[count:]
     fetch = pltpu.make_async_copy(w_hbm.at[span(own[0], words.shape[0])], words, sems.at[count])
     fetch.start()
-    fetches = row_fetches(pieces, block, sems, 0)
+    fetches = row_fetches(core, pieces, block, sems, 0)
     for other in fetches:
         other.start()
     fetch.wait()
@@ -215,12 +222,12 @@
     logits[...] = score - sq
 
 
-def score_pass(own, words, pieces, owned):
+def score_pass(core, own, words, pieces, owned):
     depth = words.shape[1]
     rows = sum(piece.shape[0] for piece in pieces)
     return pl.pallas_call(
         functools.partial(score_kernel, len(pieces)),
-        in_specs=[SMEM, HBM] + [HBM] * len(pieces),
+        in_specs=[SMEM, SMEM, HBM] + [HBM] * len(pieces),
         out_specs=VMEM,
         scratch_shapes=[
             pltpu.VMEM((rows, depth), bf16),
@@ -233,18 +240,18 @@
             flops=2 * owned * rows * depth, bytes_accessed=2 * rows * depth, transcendentals=0
         ),
         compiler_params=pltpu.CompilerParams(vmem_limit_bytes=40 * 2**20),
-    )(own, words, *pieces)
-
-
-def last_kernel(count, tile, chunk, own, w_hbm, la_ref, lse_ref, *refs):
+    )(core, own, words, *pieces)
+
+
+def last_kernel(count, tile, chunk, core, own, w_hbm, la_ref, lse_ref, *refs):
     near, direct = refs[:count], refs[count : 2 * count]
     out, block, words, assign, staged, sems, out_sems = refs[2 * count :]
     owned = words.shape[0]
     rows = la_ref.shape[1]
     fetch = pltpu.make_async_copy(w_hbm.at[span(own[0], owned)], words, sems.at[2 * count])
     fetch.start()
-    fetches = row_fetches(near, block.at[pl.ds(rows, rows)], sems, 0)
-    fetches += row_fetches(direct, block.at[pl.ds(0, rows)], sems, count)
+    fetches = row_fetches(core, near, block.at[pl.ds(rows, rows)], sems, 0)
+    fetches += row_fetches(core, direct, block.at[pl.ds(0, rows)], sems, count)
     for other in fetches:
         other.start()
     assign[:, :rows] = jnp.exp(la_ref[...] - lse_ref[0:1]).astype(bf16)
@@ -272,13 +279,13 @@
         send.wait()
 
 
-def last_pass(own, words, scored, lse, near, direct, owned, tile, chunk):
+def last_pass(core, own, words, scored, lse, near, direct, owned, tile, chunk):
     depth = words.shape[1]
     rows = scored.shape[1]
     count = len(near)
     return pl.pallas_call(
         functools.partial(last_kernel, count, tile, chunk),
-        in_specs=[SMEM, HBM, VMEM, VMEM] + [HBM] * (2 * count),
+        in_specs=[SMEM, SMEM, HBM, VMEM, VMEM] + [HBM] * (2 * count),
         out_specs=HBM,
         scratch_shapes=[
             pltpu.VMEM((2 * rows, depth), bf16),
@@ -291,7 +298,7 @@
         out_shape=jax.ShapeDtypeStruct((owned, depth), f32),
         name="last_pass",
         compiler_params=pltpu.CompilerParams(vmem_limit_bytes=50 * 2**20),
-    )(own, words, scored, lse, *near, *direct)
+    )(core, own, words, scored, lse, *near, *direct)
 
 
 def to_other(value, axis, flip):
@@ -303,22 +310,21 @@
     table = []
     for book in range(2):
         for core in range(2):
-            hop = step ^ 1 if core == 0 else step ^ 1 ^ (n // 2 - 1)
             for d in range(n):
                 here = (book * 2 + core) * n + d
-                there = ((1 - book) * 2 + core) * n + (d ^ (2 * hop))
+                there = ((1 - book) * 2 + core) * n + (d ^ (2 * step))
                 table.append((here, there))
     return lax.ppermute(value, ("pair", "code", "dp"), table)
 
 
-def hbm_named(call, *args):
-    return pltpu.with_memory_space_constraint(call(*args), pltpu.HBM)
+def in_hbm(value):
+    return pltpu.with_memory_space_constraint(value, pltpu.HBM)
 
 
 def step(samples, codebooks):
     words = pltpu.with_memory_space_constraint(codebooks[0], pltpu.HBM)
+    resident = pltpu.with_memory_space_constraint(codebooks[0], pltpu.VMEM)
     rows, _ = samples.shape
-    half = rows // 2
     n = lax.axis_size("dp")
     owned = words.shape[0] // n
     core = lax.axis_index("code").reshape(1)
@@ -329,26 +335,25 @@
     theirs = to_other(other, "code", 1)
     residual = join(core, samples, mine, theirs)
 
-    direct = [hbm_named(to_column, residual, i) for i in range(n // 2)]
-    swapped = [hbm_named(to_other, direct[i], "code", 1) for i in range(n // 2)]
-    near = [hbm_named(to_other, direct[i], "dp", 1) for i in range(n // 2)]
-    near_swapped = [hbm_named(to_other, near[i], "code", 1) for i in range(n // 2)]
-
-    lse = stats_pass(direct[0], swapped[0], words, 1024)
-    far = to_other(lse, "code", 1)
-    far = jnp.concatenate([far[:, half:], far[:, :half]], axis=1)
-    lse = jnp.logaddexp(lse, far)
+    direct = [to_column(residual, i) for i in range(n // 2)]
+    swapped = [to_other(direct[i], "code", 1) for i in range(n // 2)]
+    near = [to_other(direct[i], "dp", 1) for i in range(n // 2)]
+    near_swapped = [to_other(near[i], "code", 1) for i in range(n // 2)]
+
+    early = early_pass(resident)
+    lse = stats_pass(core, direct[0], swapped[0], resident, early, 1024)
+    lse = jnp.logaddexp(lse, to_other(lse, "code", 1))
     flip = 1
     while flip < n:
         lse = jnp.concatenate([lse, to_other(lse, "dp", flip)], axis=0)
         flip *= 2
     lse = jnp.stack([lse[0::2].reshape(-1), lse[1::2].reshape(-1)])
 
-    direct = [v for pair in zip(direct, swapped) for v in pair]
-    near = [v for pair in zip(near, near_swapped) for v in pair]
-    scored = score_pass(own, words, direct, owned)
+    direct = [in_hbm(v) for pair in zip(direct, swapped) for v in pair]
+    near = [in_hbm(v) for pair in zip(near, near_swapped) for v in pair]
+    scored = score_pass(core, own, words, direct, owned)
     updated = last_pass(
-        own, words, scored, lse, near, direct, owned, max(owned // 4, 128), 2 * rows
+        *(core, own, words, scored, lse, near, direct, owned, max(owned // 4, 128), 2 * rows),
     )
     return updated[None]
 

time: 83.4 us -> 90.1 us (1.080); the launches traced: 83.3 us -> 88.5 us
  local copies, waits for them, and re-layouts: 1.12 us -> 8.27 us
  waiting for transfers between devices: 20.4 us -> 22.4 us
  Pallas kernels: 37.9 us -> 36.3 us
  starting transfers between devices: 22.5 us -> 21 us
    unnamed x18 -> x24, local copies, waits for them, and re-layouts: 0.84 us -> 8.06 us
    ppermute x17, starting transfers between devices: 12 us -> 8.03 us  [to_other(): lax.ppermute(value, axis, [(i, i ^ flip) for i in range(lax.axis_size(axi...]
    ppermute x4, starting transfers between devices: 10.6 us -> 13 us  [to_column(): return lax.ppermute(value, ('pair', 'code', 'dp'), table)]
    ppermute x17, waiting for transfers between devices: 14.5 us -> 16.3 us  [to_other(): lax.ppermute(value, axis, [(i, i ^ flip) for i in range(lax.axis_size(axi...]
    pallas_call x1 -> x2, Pallas kernels: 10.3 us -> 8.71 us  [the longest x1 8.71 us: stats_pass(): pl.pallas_call(functools.partial(stats_kernel, tile), in_specs=[SMEM, ANY...]
  transfers between devices with their start and end apart: 21 -> 21, of which waited for: 8 -> 7; matrix products, arithmetic and copies ran while one was open for 1% -> 0% of each run, Pallas kernels for 17% -> 14%
where the time goes in v3:
time: 90.1 us; the launch traced here: 88.5 us
  Pallas kernels  36.3 us (40%)
  waiting for transfers between devices  22.4 us (25%)
  starting transfers between devices  21 us (23%)
  local copies, waits for them, and re-layouts  8.27 us (9%)
    ppermute x17, waiting for transfers between devices, to_other(): lax.ppermute(value, axis, [(i, i ^ flip) for i in range(lax.axis_size(axi...  16.3 us
    pallas_call x1, Pallas kernels, first_pass(): pl.pallas_call(functools.partial(first_kernel, tile), in_specs=[SMEM, HBM...  14.1 us
    ppermute x4, starting transfers between devices, to_column(): return lax.ppermute(value, ('pair', 'code', 'dp'), table)  13 us
    pallas_call x1, Pallas kernels, last_pass(): pl.pallas_call(functools.partial(last_kernel, count, tile, chunk), in_spe...  9.46 us
    pallas_call x1, Pallas kernels, stats_pass(): pl.pallas_call(functools.partial(stats_kernel, tile), in_specs=[SMEM, ANY...  8.71 us
    unnamed x24, local copies, waits for them, and re-layouts  8.06 us
    ppermute x17, starting transfers between devices, to_other(): lax.ppermute(value, axis, [(i, i ^ flip) for i in range(lax.axis_size(axi...  8.03 us
    ppermute x4, waiting for transfers between devices, to_column(): return lax.ppermute(value, ('pair', 'code', 'dp'), table)  6.12 us
  transfers between devices with their start and end apart: 21, of which 7 were waited for; matrix products, arithmetic and copies ran while one was open for 0% of the time, Pallas kernels for 14%

profile of v3, /device:TPU:0, one launch (start us, length us, event | category | flops | bytes accessed | tf_op | source)
XLA Modules:
  0.0 88.5 jit_solution(9930215861955553122)
XLA Ops:
  0.0 14.1 %first_pass.1 = (f32[96,1280]{1,0:T(8,128)S(1)}, f32[96,1280]{1,0:T(8,128)S(1)}) custom-call(s32[1]{0:T(128)} %bitcast.core, bf16[192,1024]{1,0:T(8,128)(2,1)} %s_hbm.1, bf16[8192,1024]{1,0:T(8,128)(2,1)} %bitcast.4), custom_call_target="tpu_custom_call" | custom-call | tf_op jit(solution)/shard_map/first_pass/pallas_call | solution.py:101
  14.1 0.6 collective-permute-start
  14.7 1.5 %collective-permute-done = f32[96,1280]{1,0:T(8,128)S(1)} collective-permute-done((f32[96,1280]{1,0:T(8,128)S(1)}, f32[96,1280]{1,0:T(8,128)S(1)}, u32[]{:S(2)}, u32[]{:S(2)}) %collective-permute-start) | collective-permute-done | bytes 491552 | tf_op jit(solution)/shard_map/ppermute | solution.py:305
  16.2 0.2 fusion.8
  16.4 0.2 subtract_convert_fusion
  16.6 2.9 %collective-permute-start.1 = (bf16[96,1024]{1,0:T(8,128)(2,1)S(1)}, bf16[96,1024]{1,0:T(8,128)(2,1)S(1)}, u32[]{:S(2)}, u32[]{:S(2)}) collective-permute-start(bf16[96,1024]{1,0:T(8,128)(2,1)S(1)} %subtract_convert_fusion), channel_id=1, source_target_pairs={{0,16},{1,17},{2,18},{3,19},{4,20},{5,21},{6,22},{7,23},{8,24},{9,... | collective-permute-start | bytes 589832 | tf_op jit(solution)/shard_map/ppermute | solution.py:317
  19.4 5.2 %collective-permute-done.1.refs_0_.a_hbm.refs_8_ = bf16[96,1024]{1,0:T(8,128)(2,1)S(1)} collective-permute-done((bf16[96,1024]{1,0:T(8,128)(2,1)S(1)}, bf16[96,1024]{1,0:T(8,128)(2,1)S(1)}, u32[]{:S(2)}, u32[]{:S(2)}) %collective-permute-start.1) | collective-permute-done | bytes 196640 | tf_op jit(solution)/shard_map/ppermute | solution.py:317
  24.6 5.8 %copy-done = bf16[1,8192,1024]{2,1,0:T(8,128)(2,1)S(1)} copy-done((bf16[1,8192,1024]{2,1,0:T(8,128)(2,1)S(1)}, bf16[1,8192,1024]{2,1,0:T(8,128)(2,1)}, u32[]{:S(2)}) %copy-start) | copy-done | bytes 16777240
  30.5 4.8 %collective-permute-start.7 = (bf16[96,1024]{1,0:T(8,128)(2,1)S(1)}, bf16[96,1024]{1,0:T(8,128)(2,1)S(1)}, u32[]{:S(2)}, u32[]{:S(2)}) collective-permute-start(bf16[96,1024]{1,0:T(8,128)(2,1)S(1)} %subtract_convert_fusion), channel_id=1, source_target_pairs={{0,22},{1,23},{2,20},{3,21},{4,18},{5,19},{6,16},{7,17},{8,30},{9,... | collective-permute-start | bytes 589832 | tf_op jit(solution)/shard_map/ppermute | solution.py:317
  35.3 1.0 %copy-done.1 = bf16[1,8192,1024]{2,1,0:T(8,128)(2,1)S(1)} copy-done((bf16[1,8192,1024]{2,1,0:T(8,128)(2,1)S(1)}, bf16[1,8192,1024]{2,1,0:T(8,128)(2,1)}, u32[]{:S(2)}) %copy-start.1) | copy-done | bytes 16777240
  36.3 8.7 %stats_pass.1 = f32[1,192]{1,0:T(1,128)S(1)} custom-call(s32[1]{0:T(128)} %bitcast.core, bf16[96,1024]{1,0:T(8,128)(2,1)S(1)} %collective-permute-done.1.refs_0_.a_hbm.refs_8_, bf16[96,1024]{1,0:T(8,128)(2,1)S(1)} %collective-permute-done.2.refs_1_.b_hbm.refs_9_, bf16[8192,1024]{1,0:T(8,128)(2,1)S(1)} %bitcast.8, bf16[16,128]{1,0:T(8,128)(2,1)S(1)} %early_pass.1.early), custom_call_target="tpu_custom_call" | custom-call | flops 3221225472 | bytes 16777216 | tf_op jit(solution)/shard_map/stats_pass/pallas_call | solution.py:182
  45.0 0.5 collective-permute-start.9
  45.5 3.8 %collective-permute-start.5 = (bf16[96,1024]{1,0:T(8,128)(2,1)S(1)}, bf16[96,1024]{1,0:T(8,128)(2,1)S(1)}, u32[]{:S(2)}, u32[]{:S(2)}) collective-permute-start(bf16[96,1024]{1,0:T(8,128)(2,1)S(1)} %subtract_convert_fusion), channel_id=1, source_target_pairs={{0,20},{1,21},{2,22},{3,23},{4,16},{5,17},{6,18},{7,19},{8,28},{9,... | collective-permute-start | bytes 589832 | tf_op jit(solution)/shard_map/ppermute | solution.py:317
  49.2 1.5 %collective-permute-start.3 = (bf16[96,1024]{1,0:T(8,128)(2,1)S(1)}, bf16[96,1024]{1,0:T(8,128)(2,1)S(1)}, u32[]{:S(2)}, u32[]{:S(2)}) collective-permute-start(bf16[96,1024]{1,0:T(8,128)(2,1)S(1)} %subtract_convert_fusion), channel_id=1, source_target_pairs={{0,18},{1,19},{2,16},{3,17},{4,22},{5,23},{6,20},{7,21},{8,26},{9,... | collective-permute-start | bytes 589832 | tf_op jit(solution)/shard_map/ppermute | solution.py:317
  50.8 1.5 %collective-permute-start.19 = (bf16[96,1024]{1,0:T(8,128)(2,1)S(1)}, bf16[96,1024]{1,0:T(8,128)(2,1)}, u32[]{:S(2)}, u32[]{:S(2)}) collective-permute-start(bf16[96,1024]{1,0:T(8,128)(2,1)S(1)} %collective-permute-done.7.refs_6_.refs_14_), channel_id=1, source_target_pairs={{0,1},{1,0},{2,3},{3,2},{4,5},{5,4},{6,7},{7,6},{8,9},{9,8},{10,11... | collective-permute-start | bytes 589832 | tf_op jit(solution)/shard_map/ppermute | solution.py:305
  52.4 0.5 collective-permute-start.10
  52.9 4.3 %collective-permute-done.10 = f32[1,192]{1,0:T(1,128)S(1)} collective-permute-done((f32[1,192]{1,0:T(1,128)S(1)}, f32[1,192]{1,0:T(1,128)S(1)}, u32[]{:S(2)}, u32[]{:S(2)}) %collective-permute-start.10) | collective-permute-done | bytes 800 | tf_op jit(solution)/shard_map/ppermute | solution.py:305
  57.2 0.5 collective-permute-start.11
  57.8 0.9 %collective-permute-done.5.refs_4_.refs_12_ = bf16[96,1024]{1,0:T(8,128)(2,1)S(1)} collective-permute-done((bf16[96,1024]{1,0:T(8,128)(2,1)S(1)}, bf16[96,1024]{1,0:T(8,128)(2,1)S(1)}, u32[]{:S(2)}, u32[]{:S(2)}) %collective-permute-start.5) | collective-permute-done | bytes 196640 | tf_op jit(solution)/shard_map/ppermute | solution.py:317
  58.7 1.6 %collective-permute-start.17 = (bf16[96,1024]{1,0:T(8,128)(2,1)S(1)}, bf16[96,1024]{1,0:T(8,128)(2,1)}, u32[]{:S(2)}, u32[]{:S(2)}) collective-permute-start(bf16[96,1024]{1,0:T(8,128)(2,1)S(1)} %collective-permute-done.5.refs_4_.refs_12_), channel_id=1, source_target_pairs={{0,1},{1,0},{2,3},{3,2},{4,5},{5,4},{6,7},{7,6},{8,9},{9,8},{10,11... | collective-permute-start | bytes 589832 | tf_op jit(solution)/shard_map/ppermute | solution.py:305
  60.3 1.2 %collective-permute-start.15 = (bf16[96,1024]{1,0:T(8,128)(2,1)S(1)}, bf16[96,1024]{1,0:T(8,128)(2,1)}, u32[]{:S(2)}, u32[]{:S(2)}) collective-permute-start(bf16[96,1024]{1,0:T(8,128)(2,1)S(1)} %collective-permute-done.3.refs_2_.refs_10_), channel_id=1, source_target_pairs={{0,1},{1,0},{2,3},{3,2},{4,5},{5,4},{6,7},{7,6},{8,9},{9,8},{10,11... | collective-permute-start | bytes 589832 | tf_op jit(solution)/shard_map/ppermute | solution.py:305
  61.5 0.9 %collective-permute-start.13 = (bf16[96,1024]{1,0:T(8,128)(2,1)S(1)}, bf16[96,1024]{1,0:T(8,128)(2,1)}, u32[]{:S(2)}, u32[]{:S(2)}) collective-permute-start(bf16[96,1024]{1,0:T(8,128)(2,1)S(1)} %collective-permute-done.1.refs_0_.a_hbm.refs_8_), channel_id=1, source_target_pairs={{0,1},{1,0},{2,3},{3,2},{4,5},{5,4},{6,7},{7,6},{8,9},{9,8},{10,11... | collective-permute-start | bytes 589832 | tf_op jit(solution)/shard_map/ppermute | solution.py:305
  62.5 4.1 %collective-permute-done.17.refs_4_ = bf16[96,1024]{1,0:T(8,128)(2,1)} collective-permute-done((bf16[96,1024]{1,0:T(8,128)(2,1)S(1)}, bf16[96,1024]{1,0:T(8,128)(2,1)}, u32[]{:S(2)}, u32[]{:S(2)}) %collective-permute-start.17) | collective-permute-done | bytes 196640 | tf_op jit(solution)/shard_map/ppermute | solution.py:305
  66.5 0.5 collective-permute-start.18
  67.1 3.7 %collective-permute-done.15.refs_2_ = bf16[96,1024]{1,0:T(8,128)(2,1)} collective-permute-done((bf16[96,1024]{1,0:T(8,128)(2,1)S(1)}, bf16[96,1024]{1,0:T(8,128)(2,1)}, u32[]{:S(2)}, u32[]{:S(2)}) %collective-permute-start.15) | collective-permute-done | bytes 196640 | tf_op jit(solution)/shard_map/ppermute | solution.py:305
  70.8 2.7 %collective-permute-done.13.refs_0_ = bf16[96,1024]{1,0:T(8,128)(2,1)} collective-permute-done((bf16[96,1024]{1,0:T(8,128)(2,1)S(1)}, bf16[96,1024]{1,0:T(8,128)(2,1)}, u32[]{:S(2)}, u32[]{:S(2)}) %collective-permute-start.13) | collective-permute-done | bytes 196640 | tf_op jit(solution)/shard_map/ppermute | solution.py:305
  73.6 0.6 copy-done.10
  74.1 4.0 %score_pass.1.la_ref = f32[1024,768]{1,0:T(8,128)S(1)} custom-call(s32[1]{0:T(128)} %bitcast.core, s32[1]{0:T(128)} %bitcast.1.own, bf16[8192,1024]{1,0:T(8,128)(2,1)} %bitcast.5, bf16[96,1024]{1,0:T(8,128)(2,1)} %copy-done.2, bf16[96,1024]{1,0:T(8,128)(2,1)} %copy-done.3, bf16[96,1024]{1,0:T(8,128)(2,1)} %copy-done.7, bf16[96,1024]{1,0:T(8,128)(2,1)} %copy-done.10, ...), custom_call_target="tpu_custom_call" | custom-call | flops 1610612736 | bytes 1572864 | tf_op jit(solution)/shard_map/score_pass/pallas_call | solution.py:228
  78.2 0.1 stack_reshape.6
  78.3 0.1 stack_reshape.7
  78.4 0.7 copy-done.11
  79.1 9.5 %last_pass.1 = f32[1024,1024]{1,0:T(8,128)} custom-call(s32[1]{0:T(128)} %bitcast.core, s32[1]{0:T(128)} %bitcast.1.own, bf16[8192,1024]{1,0:T(8,128)(2,1)} %bitcast.6, f32[1024,768]{1,0:T(8,128)S(1)} %score_pass.1.la_ref, f32[2,768]{1,0:T(2,128)S(1)} %pad_maximum_fusion.1.lse_ref, bf16[96,1024]{1,0:T(8,128)(2,1)} %collective-permute-done.13.refs_0_, ...), custom_call_target="tpu_custom_call" | custom-call | tf_op jit(solution)/shard_map/last_pass/pallas_call | solution.py:286
  (50 shorter events, 0.3 us)
Async XLA Ops:
  0.0 16.4 %copy-start.4 = (bf16[192,1024]{1,0:T(8,128)(2,1)S(1)}, bf16[192,1024]{1,0:T(8,128)(2,1)}, u32[]{:S(2)}) copy-start(bf16[192,1024]{1,0:T(8,128)(2,1)} %s_hbm.1) | copy-start | bytes 1179652
  14.1 2.1 %collective-permute-start = (f32[96,1280]{1,0:T(8,128)S(1)}, f32[96,1280]{1,0:T(8,128)S(1)}, u32[]{:S(2)}, u32[]{:S(2)}) collective-permute-start(f32[96,1280]{1,0:T(8,128)S(1)} %get-tuple-element.8), channel_id=1, source_target_pairs={{0,8},{8,0},{1,9},{9,1},{2,10},{10,2},{3,11},{11,3},{4,12},{12,4},... | collective-permute-start | bytes 1474568 | tf_op jit(solution)/shard_map/ppermute | solution.py:305
  16.6 8.1 %collective-permute-start.1 = (bf16[96,1024]{1,0:T(8,128)(2,1)S(1)}, bf16[96,1024]{1,0:T(8,128)(2,1)S(1)}, u32[]{:S(2)}, u32[]{:S(2)}) collective-permute-start(bf16[96,1024]{1,0:T(8,128)(2,1)S(1)} %subtract_convert_fusion), channel_id=1, source_target_pairs={{0,16},{1,17},{2,18},{3,19},{4,20},{5,21},{6,22},{7,23},{8,24},{9,... | collective-permute-start | bytes 589832 | tf_op jit(solution)/shard_map/ppermute | solution.py:317
  24.6 36.9 %copy-start.2 = (bf16[96,1024]{1,0:T(8,128)(2,1)}, bf16[96,1024]{1,0:T(8,128)(2,1)S(1)}, u32[]{:S(2)}) copy-start(bf16[96,1024]{1,0:T(8,128)(2,1)S(1)} %collective-permute-done.1.refs_0_.a_hbm.refs_8_) | copy-start | bytes 589828
  24.6 10.7 %collective-permute-start.2 = (bf16[96,1024]{1,0:T(8,128)(2,1)S(1)}, bf16[96,1024]{1,0:T(8,128)(2,1)S(1)}, u32[]{:S(2)}, u32[]{:S(2)}) collective-permute-start(bf16[96,1024]{1,0:T(8,128)(2,1)S(1)} %collective-permute-done.1.refs_0_.a_hbm.refs_8_), channel_id=1, source_target_pairs={{0,8},{8,0},{1,9},{9,1},{2,10},{10,2},{3,11},{11,3},{4,12},{12,4},... | collective-permute-start | bytes 589832 | tf_op jit(solution)/shard_map/ppermute | solution.py:305
  24.6 5.8 %copy-start = (bf16[1,8192,1024]{2,1,0:T(8,128)(2,1)S(1)}, bf16[1,8192,1024]{2,1,0:T(8,128)(2,1)}, u32[]{:S(2)}) copy-start(bf16[1,8192,1024]{2,1,0:T(8,128)(2,1)} %param.3) | copy-start | bytes 50331652
  30.5 5.8 %copy-start.1 = (bf16[1,8192,1024]{2,1,0:T(8,128)(2,1)S(1)}, bf16[1,8192,1024]{2,1,0:T(8,128)(2,1)}, u32[]{:S(2)}) copy-start(bf16[1,8192,1024]{2,1,0:T(8,128)(2,1)} %param.3) | copy-start | bytes 50331652
  30.5 20.3 %collective-permute-start.7 = (bf16[96,1024]{1,0:T(8,128)(2,1)S(1)}, bf16[96,1024]{1,0:T(8,128)(2,1)S(1)}, u32[]{:S(2)}, u32[]{:S(2)}) collective-permute-start(bf16[96,1024]{1,0:T(8,128)(2,1)S(1)} %subtract_convert_fusion), channel_id=1, source_target_pairs={{0,22},{1,23},{2,20},{3,21},{4,18},{5,19},{6,16},{7,17},{8,30},{9,... | collective-permute-start | bytes 589832 | tf_op jit(solution)/shard_map/ppermute | solution.py:317
  36.2 8.7 %copy-start.3 = (bf16[96,1024]{1,0:T(8,128)(2,1)}, bf16[96,1024]{1,0:T(8,128)(2,1)S(1)}, u32[]{:S(2)}) copy-start(bf16[96,1024]{1,0:T(8,128)(2,1)S(1)} %collective-permute-done.2.refs_1_.b_hbm.refs_9_) | copy-start | bytes 589828
  45.0 7.4 %collective-permute-start.9 = (f32[1,192]{1,0:T(1,128)S(1)}, f32[1,192]{1,0:T(1,128)S(1)}, u32[]{:S(2)}, u32[]{:S(2)}) collective-permute-start(f32[1,192]{1,0:T(1,128)S(1)} %stats_pass.1), channel_id=1, source_target_pairs={{0,8},{8,0},{1,9},{9,1},{2,10},{10,2},{3,11},{11,3},{4,12},{12,4},... | collective-permute-start | bytes 2312 | tf_op jit(solution)/shard_map/ppermute | solution.py:305
  45.5 13.2 %collective-permute-start.5 = (bf16[96,1024]{1,0:T(8,128)(2,1)S(1)}, bf16[96,1024]{1,0:T(8,128)(2,1)S(1)}, u32[]{:S(2)}, u32[]{:S(2)}) collective-permute-start(bf16[96,1024]{1,0:T(8,128)(2,1)S(1)} %subtract_convert_fusion), channel_id=1, source_target_pairs={{0,20},{1,21},{2,22},{3,23},{4,16},{5,17},{6,18},{7,19},{8,28},{9,... | collective-permute-start | bytes 589832 | tf_op jit(solution)/shard_map/ppermute | solution.py:317
  49.2 11.0 %collective-permute-start.3 = (bf16[96,1024]{1,0:T(8,128)(2,1)S(1)}, bf16[96,1024]{1,0:T(8,128)(2,1)S(1)}, u32[]{:S(2)}, u32[]{:S(2)}) collective-permute-start(bf16[96,1024]{1,0:T(8,128)(2,1)S(1)} %subtract_convert_fusion), channel_id=1, source_target_pairs={{0,18},{1,19},{2,16},{3,17},{4,22},{5,23},{6,20},{7,21},{8,26},{9,... | collective-permute-start | bytes 589832 | tf_op jit(solution)/shard_map/ppermute | solution.py:317
  50.8 11.7 %copy-start.5 = (bf16[96,1024]{1,0:T(8,128)(2,1)}, bf16[96,1024]{1,0:T(8,128)(2,1)S(1)}, u32[]{:S(2)}) copy-start(bf16[96,1024]{1,0:T(8,128)(2,1)S(1)} %collective-permute-done.7.refs_6_.refs_14_) | copy-start | bytes 589828
  50.8 9.5 %collective-permute-start.19 = (bf16[96,1024]{1,0:T(8,128)(2,1)S(1)}, bf16[96,1024]{1,0:T(8,128)(2,1)}, u32[]{:S(2)}, u32[]{:S(2)}) collective-permute-start(bf16[96,1024]{1,0:T(8,128)(2,1)S(1)} %collective-permute-done.7.refs_6_.refs_14_), channel_id=1, source_target_pairs={{0,1},{1,0},{2,3},{3,2},{4,5},{5,4},{6,7},{7,6},{8,9},{9,8},{10,11... | collective-permute-start | bytes 589832 | tf_op jit(solution)/shard_map/ppermute | solution.py:305
  52.3 9.2 %collective-permute-start.8 = (bf16[96,1024]{1,0:T(8,128)(2,1)S(1)}, bf16[96,1024]{1,0:T(8,128)(2,1)S(1)}, u32[]{:S(2)}, u32[]{:S(2)}) collective-permute-start(bf16[96,1024]{1,0:T(8,128)(2,1)S(1)} %collective-permute-done.7.refs_6_.refs_14_), channel_id=1, source_target_pairs={{0,8},{8,0},{1,9},{9,1},{2,10},{10,2},{3,11},{11,3},{4,12},{12,4},... | collective-permute-start | bytes 589832 | tf_op jit(solution)/shard_map/ppermute | solution.py:305
  52.4 4.9 %collective-permute-start.10 = (f32[1,192]{1,0:T(1,128)S(1)}, f32[1,192]{1,0:T(1,128)S(1)}, u32[]{:S(2)}, u32[]{:S(2)}) collective-permute-start(f32[1,192]{1,0:T(1,128)S(1)} %compare_select_fusion), channel_id=1, source_target_pairs={{0,1},{1,0},{2,3},{3,2},{4,5},{5,4},{6,7},{7,6},{8,9},{9,8},{10,11... | collective-permute-start | bytes 2312 | tf_op jit(solution)/shard_map/ppermute | solution.py:305
  57.2 5.2 %collective-permute-start.11 = (f32[2,192]{1,0:T(2,128)S(1)}, f32[2,192]{1,0:T(2,128)S(1)}, u32[]{:S(2)}, u32[]{:S(2)}) collective-permute-start(f32[2,192]{1,0:T(2,128)S(1)} %pad_maximum_fusion.3), channel_id=1, source_target_pairs={{0,2},{1,3},{2,0},{3,1},{4,6},{5,7},{6,4},{7,5},{8,10},{9,11},{10,... | collective-permute-start | bytes 4616 | tf_op jit(solution)/shard_map/ppermute | solution.py:305
  58.7 15.4 %copy-start.6 = (bf16[96,1024]{1,0:T(8,128)(2,1)}, bf16[96,1024]{1,0:T(8,128)(2,1)S(1)}, u32[]{:S(2)}) copy-start(bf16[96,1024]{1,0:T(8,128)(2,1)S(1)} %collective-permute-done.5.refs_4_.refs_12_) | copy-start | bytes 589828
  58.7 7.8 %collective-permute-start.17 = (bf16[96,1024]{1,0:T(8,128)(2,1)S(1)}, bf16[96,1024]{1,0:T(8,128)(2,1)}, u32[]{:S(2)}, u32[]{:S(2)}) collective-permute-start(bf16[96,1024]{1,0:T(8,128)(2,1)S(1)} %collective-permute-done.5.refs_4_.refs_12_), channel_id=1, source_target_pairs={{0,1},{1,0},{2,3},{3,2},{4,5},{5,4},{6,7},{7,6},{8,9},{9,8},{10,11... | collective-permute-start | bytes 589832 | tf_op jit(solution)/shard_map/ppermute | solution.py:305
  60.3 13.3 %copy-start.7 = (bf16[96,1024]{1,0:T(8,128)(2,1)}, bf16[96,1024]{1,0:T(8,128)(2,1)S(1)}, u32[]{:S(2)}) copy-start(bf16[96,1024]{1,0:T(8,128)(2,1)S(1)} %collective-permute-done.3.refs_2_.refs_10_) | copy-start | bytes 589828
  60.3 6.3 %collective-permute-start.6 = (bf16[96,1024]{1,0:T(8,128)(2,1)S(1)}, bf16[96,1024]{1,0:T(8,128)(2,1)S(1)}, u32[]{:S(2)}, u32[]{:S(2)}) collective-permute-start(bf16[96,1024]{1,0:T(8,128)(2,1)S(1)} %collective-permute-done.5.refs_4_.refs_12_), channel_id=1, source_target_pairs={{0,8},{8,0},{1,9},{9,1},{2,10},{10,2},{3,11},{11,3},{4,12},{12,4},... | collective-permute-start | bytes 589832 | tf_op jit(solution)/shard_map/ppermute | solution.py:305
  60.3 10.5 %collective-permute-start.15 = (bf16[96,1024]{1,0:T(8,128)(2,1)S(1)}, bf16[96,1024]{1,0:T(8,128)(2,1)}, u32[]{:S(2)}, u32[]{:S(2)}) collective-permute-start(bf16[96,1024]{1,0:T(8,128)(2,1)S(1)} %collective-permute-done.3.refs_2_.refs_10_), channel_id=1, source_target_pairs={{0,1},{1,0},{2,3},{3,2},{4,5},{5,4},{6,7},{7,6},{8,9},{9,8},{10,11... | collective-permute-start | bytes 589832 | tf_op jit(solution)/shard_map/ppermute | solution.py:305
  61.5 12.0 %copy-start.8 = (bf16[96,1024]{1,0:T(8,128)(2,1)}, bf16[96,1024]{1,0:T(8,128)(2,1)S(1)}, u32[]{:S(2)}) copy-start(bf16[96,1024]{1,0:T(8,128)(2,1)S(1)} %collective-permute-done.8.refs_7_.refs_15_) | copy-start | bytes 589828
  61.5 11.9 %collective-permute-start.13 = (bf16[96,1024]{1,0:T(8,128)(2,1)S(1)}, bf16[96,1024]{1,0:T(8,128)(2,1)}, u32[]{:S(2)}, u32[]{:S(2)}) collective-permute-start(bf16[96,1024]{1,0:T(8,128)(2,1)S(1)} %collective-permute-done.1.refs_0_.a_hbm.refs_8_), channel_id=1, source_target_pairs={{0,1},{1,0},{2,3},{3,2},{4,5},{5,4},{6,7},{7,6},{8,9},{9,8},{10,11... | collective-permute-start | bytes 589832 | tf_op jit(solution)/shard_map/ppermute | solution.py:305
  62.4 11.0 %collective-permute-start.4 = (bf16[96,1024]{1,0:T(8,128)(2,1)S(1)}, bf16[96,1024]{1,0:T(8,128)(2,1)S(1)}, u32[]{:S(2)}, u32[]{:S(2)}) collective-permute-start(bf16[96,1024]{1,0:T(8,128)(2,1)S(1)} %collective-permute-done.3.refs_2_.refs_10_), channel_id=1, source_target_pairs={{0,8},{8,0},{1,9},{9,1},{2,10},{10,2},{3,11},{11,3},{4,12},{12,4},... | collective-permute-start | bytes 589832 | tf_op jit(solution)/shard_map/ppermute | solution.py:305
  66.5 11.8 %collective-permute-start.20 = (bf16[96,1024]{1,0:T(8,128)(2,1)}, bf16[96,1024]{1,0:T(8,128)(2,1)}, u32[]{:S(2)}, u32[]{:S(2)}) collective-permute-start(bf16[96,1024]{1,0:T(8,128)(2,1)} %collective-permute-done.19.refs_6_), channel_id=1, source_target_pairs={{0,8},{8,0},{1,9},{9,1},{2,10},{10,2},{3,11},{11,3},{4,12},{12,4},... | collective-permute-start | bytes 589832 | tf_op jit(solution)/shard_map/ppermute | solution.py:305
  66.5 7.0 %copy-start.9 = (bf16[96,1024]{1,0:T(8,128)(2,1)}, bf16[96,1024]{1,0:T(8,128)(2,1)S(1)}, u32[]{:S(2)}) copy-start(bf16[96,1024]{1,0:T(8,128)(2,1)S(1)} %collective-permute-done.6.refs_5_.refs_13_) | copy-start | bytes 589828
  66.5 11.8 %collective-permute-start.18 = (bf16[96,1024]{1,0:T(8,128)(2,1)}, bf16[96,1024]{1,0:T(8,128)(2,1)}, u32[]{:S(2)}, u32[]{:S(2)}) collective-permute-start(bf16[96,1024]{1,0:T(8,128)(2,1)} %collective-permute-done.17.refs_4_), channel_id=1, source_target_pairs={{0,8},{8,0},{1,9},{9,1},{2,10},{10,2},{3,11},{11,3},{4,12},{12,4},... | collective-permute-start | bytes 589832 | tf_op jit(solution)/shard_map/ppermute | solution.py:305
  70.7 7.6 %collective-permute-start.16 = (bf16[96,1024]{1,0:T(8,128)(2,1)}, bf16[96,1024]{1,0:T(8,128)(2,1)}, u32[]{:S(2)}, u32[]{:S(2)}) collective-permute-start(bf16[96,1024]{1,0:T(8,128)(2,1)} %collective-permute-done.15.refs_2_), channel_id=1, source_target_pairs={{0,8},{8,0},{1,9},{9,1},{2,10},{10,2},{3,11},{11,3},{4,12},{12,4},... | collective-permute-start | bytes 589832 | tf_op jit(solution)/shard_map/ppermute | solution.py:305
  73.4 5.0 %collective-permute-start.14 = (bf16[96,1024]{1,0:T(8,128)(2,1)}, bf16[96,1024]{1,0:T(8,128)(2,1)S(1)}, u32[]{:S(2)}, u32[]{:S(2)}) collective-permute-start(bf16[96,1024]{1,0:T(8,128)(2,1)} %collective-permute-done.13.refs_0_), channel_id=1, source_target_pairs={{0,8},{8,0},{1,9},{9,1},{2,10},{10,2},{3,11},{11,3},{4,12},{12,4},... | collective-permute-start | bytes 589832 | tf_op jit(solution)/shard_map/ppermute | solution.py:305
  73.4 0.7 copy-start.10
  73.4 4.7 %collective-permute-start.12 = (f32[4,192]{1,0:T(4,128)S(1)}, f32[4,192]{1,0:T(4,128)S(1)}, u32[]{:S(2)}, u32[]{:S(2)}) collective-permute-start(f32[4,192]{1,0:T(4,128)S(1)} %pad_maximum_fusion.2), channel_id=1, source_target_pairs={{0,4},{1,5},{2,6},{3,7},{4,0},{5,1},{6,2},{7,3},{8,12},{9,13},{10,... | collective-permute-start | bytes 9224 | tf_op jit(solution)/shard_map/ppermute | solution.py:305
  (1 other events, 0.7 us)

commit v4 on v3

--- a/solution.py
+++ b/solution.py
@@ -252,10 +252,12 @@
     fetch.start()
     fetches = row_fetches(core, near, block.at[pl.ds(rows, rows)], sems, 0)
     fetches += row_fetches(core, direct, block.at[pl.ds(0, rows)], sems, count)
-    for other in fetches:
+    for other in fetches[:count]:
         other.start()
     assign[:, :rows] = jnp.exp(la_ref[...] - lse_ref[0:1]).astype(bf16)
     fetch.wait()
+    for other in fetches[count:]:
+        other.start()
     sq = square_sums(words[...])
     twice = words[...] * 2
     each = near[0].shape[0]
@@ -353,7 +355,7 @@
     near = [in_hbm(v) for pair in zip(near, near_swapped) for v in pair]
     scored = score_pass(core, own, words, direct, owned)
     updated = last_pass(
-        *(core, own, words, scored, lse, near, direct, owned, max(owned // 4, 128), 2 * rows),
+        *(core, own, words, scored, lse, near, direct, owned, max(owned // 8, 128), 2 * rows),
     )
     return updated[None]
 

time: 90.1 us -> 90 us (level)
  no operation moved by 1% of the time
where the time goes in v4:
time: 90 us; the launch traced here: 88.4 us
  Pallas kernels  36.1 us (40%)
  waiting for transfers between devices  22.4 us (25%)
  starting transfers between devices  21 us (23%)
  local copies, waits for them, and re-layouts  8.27 us (9%)
    ppermute x17, waiting for transfers between devices, to_other(): lax.ppermute(value, axis, [(i, i ^ flip) for i in range(lax.axis_size(axi...  16.3 us
    pallas_call x1, Pallas kernels, first_pass(): pl.pallas_call(functools.partial(first_kernel, tile), in_specs=[SMEM, HBM...  14.1 us
    ppermute x4, starting transfers between devices, to_column(): return lax.ppermute(value, ('pair', 'code', 'dp'), table)  13 us
    pallas_call x1, Pallas kernels, last_pass(): pl.pallas_call(functools.partial(last_kernel, count, tile, chunk), in_spe...  9.29 us
    pallas_call x1, Pallas kernels, stats_pass(): pl.pallas_call(functools.partial(stats_kernel, tile), in_specs=[SMEM, ANY...  8.71 us
    unnamed x24, local copies, waits for them, and re-layouts  8.06 us
    ppermute x17, starting transfers between devices, to_other(): lax.ppermute(value, axis, [(i, i ^ flip) for i in range(lax.axis_size(axi...  8.03 us
    ppermute x4, waiting for transfers between devices, to_column(): return lax.ppermute(value, ('pair', 'code', 'dp'), table)  6.12 us
  transfers between devices with their start and end apart: 21, of which 7 were waited for; matrix products, arithmetic and copies ran while one was open for 0% of the time, Pallas kernels for 14%

profile of v4, /device:TPU:0, one launch (start us, length us, event | category | flops | bytes accessed | tf_op | source)
XLA Modules:
  0.0 88.4 jit_solution(3642552110759445239)
XLA Ops:
  0.0 14.1 %first_pass.1 = (f32[96,1280]{1,0:T(8,128)S(1)}, f32[96,1280]{1,0:T(8,128)S(1)}) custom-call(s32[1]{0:T(128)} %bitcast.core, bf16[192,1024]{1,0:T(8,128)(2,1)} %s_hbm.1, bf16[8192,1024]{1,0:T(8,128)(2,1)} %bitcast.4), custom_call_target="tpu_custom_call" | custom-call | tf_op jit(solution)/shard_map/first_pass/pallas_call | solution.py:101
  14.1 0.6 collective-permute-start
  14.7 1.5 %collective-permute-done = f32[96,1280]{1,0:T(8,128)S(1)} collective-permute-done((f32[96,1280]{1,0:T(8,128)S(1)}, f32[96,1280]{1,0:T(8,128)S(1)}, u32[]{:S(2)}, u32[]{:S(2)}) %collective-permute-start) | collective-permute-done | bytes 491552 | tf_op jit(solution)/shard_map/ppermute | solution.py:307
  16.2 0.2 fusion.8
  16.4 0.2 subtract_convert_fusion
  16.6 2.9 %collective-permute-start.1 = (bf16[96,1024]{1,0:T(8,128)(2,1)S(1)}, bf16[96,1024]{1,0:T(8,128)(2,1)S(1)}, u32[]{:S(2)}, u32[]{:S(2)}) collective-permute-start(bf16[96,1024]{1,0:T(8,128)(2,1)S(1)} %subtract_convert_fusion), channel_id=1, source_target_pairs={{0,16},{1,17},{2,18},{3,19},{4,20},{5,21},{6,22},{7,23},{8,24},{9,... | collective-permute-start | bytes 589832 | tf_op jit(solution)/shard_map/ppermute | solution.py:319
  19.4 5.2 %collective-permute-done.1.refs_0_.a_hbm.refs_8_ = bf16[96,1024]{1,0:T(8,128)(2,1)S(1)} collective-permute-done((bf16[96,1024]{1,0:T(8,128)(2,1)S(1)}, bf16[96,1024]{1,0:T(8,128)(2,1)S(1)}, u32[]{:S(2)}, u32[]{:S(2)}) %collective-permute-start.1) | collective-permute-done | bytes 196640 | tf_op jit(solution)/shard_map/ppermute | solution.py:319
  24.6 5.8 %copy-done = bf16[1,8192,1024]{2,1,0:T(8,128)(2,1)S(1)} copy-done((bf16[1,8192,1024]{2,1,0:T(8,128)(2,1)S(1)}, bf16[1,8192,1024]{2,1,0:T(8,128)(2,1)}, u32[]{:S(2)}) %copy-start) | copy-done | bytes 16777240
  30.5 4.8 %collective-permute-start.7 = (bf16[96,1024]{1,0:T(8,128)(2,1)S(1)}, bf16[96,1024]{1,0:T(8,128)(2,1)S(1)}, u32[]{:S(2)}, u32[]{:S(2)}) collective-permute-start(bf16[96,1024]{1,0:T(8,128)(2,1)S(1)} %subtract_convert_fusion), channel_id=1, source_target_pairs={{0,22},{1,23},{2,20},{3,21},{4,18},{5,19},{6,16},{7,17},{8,30},{9,... | collective-permute-start | bytes 589832 | tf_op jit(solution)/shard_map/ppermute | solution.py:319
  35.3 1.0 %copy-done.1 = bf16[1,8192,1024]{2,1,0:T(8,128)(2,1)S(1)} copy-done((bf16[1,8192,1024]{2,1,0:T(8,128)(2,1)S(1)}, bf16[1,8192,1024]{2,1,0:T(8,128)(2,1)}, u32[]{:S(2)}) %copy-start.1) | copy-done | bytes 16777240
  36.3 8.7 %stats_pass.1 = f32[1,192]{1,0:T(1,128)S(1)} custom-call(s32[1]{0:T(128)} %bitcast.core, bf16[96,1024]{1,0:T(8,128)(2,1)S(1)} %collective-permute-done.1.refs_0_.a_hbm.refs_8_, bf16[96,1024]{1,0:T(8,128)(2,1)S(1)} %collective-permute-done.2.refs_1_.b_hbm.refs_9_, bf16[8192,1024]{1,0:T(8,128)(2,1)S(1)} %bitcast.8, bf16[16,128]{1,0:T(8,128)(2,1)S(1)} %early_pass.1.early), custom_call_target="tpu_custom_call" | custom-call | flops 3221225472 | bytes 16777216 | tf_op jit(solution)/shard_map/stats_pass/pallas_call | solution.py:182
  45.0 0.5 collective-permute-start.9
  45.5 3.8 %collective-permute-start.5 = (bf16[96,1024]{1,0:T(8,128)(2,1)S(1)}, bf16[96,1024]{1,0:T(8,128)(2,1)S(1)}, u32[]{:S(2)}, u32[]{:S(2)}) collective-permute-start(bf16[96,1024]{1,0:T(8,128)(2,1)S(1)} %subtract_convert_fusion), channel_id=1, source_target_pairs={{0,20},{1,21},{2,22},{3,23},{4,16},{5,17},{6,18},{7,19},{8,28},{9,... | collective-permute-start | bytes 589832 | tf_op jit(solution)/shard_map/ppermute | solution.py:319
  49.2 1.5 %collective-permute-start.3 = (bf16[96,1024]{1,0:T(8,128)(2,1)S(1)}, bf16[96,1024]{1,0:T(8,128)(2,1)S(1)}, u32[]{:S(2)}, u32[]{:S(2)}) collective-permute-start(bf16[96,1024]{1,0:T(8,128)(2,1)S(1)} %subtract_convert_fusion), channel_id=1, source_target_pairs={{0,18},{1,19},{2,16},{3,17},{4,22},{5,23},{6,20},{7,21},{8,26},{9,... | collective-permute-start | bytes 589832 | tf_op jit(solution)/shard_map/ppermute | solution.py:319
  50.8 1.5 %collective-permute-start.19 = (bf16[96,1024]{1,0:T(8,128)(2,1)S(1)}, bf16[96,1024]{1,0:T(8,128)(2,1)}, u32[]{:S(2)}, u32[]{:S(2)}) collective-permute-start(bf16[96,1024]{1,0:T(8,128)(2,1)S(1)} %collective-permute-done.7.refs_6_.refs_14_), channel_id=1, source_target_pairs={{0,1},{1,0},{2,3},{3,2},{4,5},{5,4},{6,7},{7,6},{8,9},{9,8},{10,11... | collective-permute-start | bytes 589832 | tf_op jit(solution)/shard_map/ppermute | solution.py:307
  52.4 0.5 collective-permute-start.10
  52.9 4.3 %collective-permute-done.10 = f32[1,192]{1,0:T(1,128)S(1)} collective-permute-done((f32[1,192]{1,0:T(1,128)S(1)}, f32[1,192]{1,0:T(1,128)S(1)}, u32[]{:S(2)}, u32[]{:S(2)}) %collective-permute-start.10) | collective-permute-done | bytes 800 | tf_op jit(solution)/shard_map/ppermute | solution.py:307
  57.2 0.5 collective-permute-start.11
  57.8 0.9 %collective-permute-done.5.refs_4_.refs_12_ = bf16[96,1024]{1,0:T(8,128)(2,1)S(1)} collective-permute-done((bf16[96,1024]{1,0:T(8,128)(2,1)S(1)}, bf16[96,1024]{1,0:T(8,128)(2,1)S(1)}, u32[]{:S(2)}, u32[]{:S(2)}) %collective-permute-start.5) | collective-permute-done | bytes 196640 | tf_op jit(solution)/shard_map/ppermute | solution.py:319
  58.7 1.6 %collective-permute-start.17 = (bf16[96,1024]{1,0:T(8,128)(2,1)S(1)}, bf16[96,1024]{1,0:T(8,128)(2,1)}, u32[]{:S(2)}, u32[]{:S(2)}) collective-permute-start(bf16[96,1024]{1,0:T(8,128)(2,1)S(1)} %collective-permute-done.5.refs_4_.refs_12_), channel_id=1, source_target_pairs={{0,1},{1,0},{2,3},{3,2},{4,5},{5,4},{6,7},{7,6},{8,9},{9,8},{10,11... | collective-permute-start | bytes 589832 | tf_op jit(solution)/shard_map/ppermute | solution.py:307
  60.3 1.2 %collective-permute-start.15 = (bf16[96,1024]{1,0:T(8,128)(2,1)S(1)}, bf16[96,1024]{1,0:T(8,128)(2,1)}, u32[]{:S(2)}, u32[]{:S(2)}) collective-permute-start(bf16[96,1024]{1,0:T(8,128)(2,1)S(1)} %collective-permute-done.3.refs_2_.refs_10_), channel_id=1, source_target_pairs={{0,1},{1,0},{2,3},{3,2},{4,5},{5,4},{6,7},{7,6},{8,9},{9,8},{10,11... | collective-permute-start | bytes 589832 | tf_op jit(solution)/shard_map/ppermute | solution.py:307
  61.5 0.9 %collective-permute-start.13 = (bf16[96,1024]{1,0:T(8,128)(2,1)S(1)}, bf16[96,1024]{1,0:T(8,128)(2,1)}, u32[]{:S(2)}, u32[]{:S(2)}) collective-permute-start(bf16[96,1024]{1,0:T(8,128)(2,1)S(1)} %collective-permute-done.1.refs_0_.a_hbm.refs_8_), channel_id=1, source_target_pairs={{0,1},{1,0},{2,3},{3,2},{4,5},{5,4},{6,7},{7,6},{8,9},{9,8},{10,11... | collective-permute-start | bytes 589832 | tf_op jit(solution)/shard_map/ppermute | solution.py:307
  62.5 4.1 %collective-permute-done.17.refs_4_ = bf16[96,1024]{1,0:T(8,128)(2,1)} collective-permute-done((bf16[96,1024]{1,0:T(8,128)(2,1)S(1)}, bf16[96,1024]{1,0:T(8,128)(2,1)}, u32[]{:S(2)}, u32[]{:S(2)}) %collective-permute-start.17) | collective-permute-done | bytes 196640 | tf_op jit(solution)/shard_map/ppermute | solution.py:307
  66.5 0.5 collective-permute-start.18
  67.1 3.7 %collective-permute-done.15.refs_2_ = bf16[96,1024]{1,0:T(8,128)(2,1)} collective-permute-done((bf16[96,1024]{1,0:T(8,128)(2,1)S(1)}, bf16[96,1024]{1,0:T(8,128)(2,1)}, u32[]{:S(2)}, u32[]{:S(2)}) %collective-permute-start.15) | collective-permute-done | bytes 196640 | tf_op jit(solution)/shard_map/ppermute | solution.py:307
  70.8 2.7 %collective-permute-done.13.refs_0_ = bf16[96,1024]{1,0:T(8,128)(2,1)} collective-permute-done((bf16[96,1024]{1,0:T(8,128)(2,1)S(1)}, bf16[96,1024]{1,0:T(8,128)(2,1)}, u32[]{:S(2)}, u32[]{:S(2)}) %collective-permute-start.13) | collective-permute-done | bytes 196640 | tf_op jit(solution)/shard_map/ppermute | solution.py:307
  73.6 0.6 copy-done.10
  74.1 4.0 %score_pass.1.la_ref = f32[1024,768]{1,0:T(8,128)S(1)} custom-call(s32[1]{0:T(128)} %bitcast.core, s32[1]{0:T(128)} %bitcast.1.own, bf16[8192,1024]{1,0:T(8,128)(2,1)} %bitcast.5, bf16[96,1024]{1,0:T(8,128)(2,1)} %copy-done.2, bf16[96,1024]{1,0:T(8,128)(2,1)} %copy-done.3, bf16[96,1024]{1,0:T(8,128)(2,1)} %copy-done.7, bf16[96,1024]{1,0:T(8,128)(2,1)} %copy-done.10, ...), custom_call_target="tpu_custom_call" | custom-call | flops 1610612736 | bytes 1572864 | tf_op jit(solution)/shard_map/score_pass/pallas_call | solution.py:228
  78.2 0.1 stack_reshape.6
  78.3 0.1 stack_reshape.7
  78.4 0.7 copy-done.11
  79.1 9.3 %last_pass.1 = f32[1024,1024]{1,0:T(8,128)} custom-call(s32[1]{0:T(128)} %bitcast.core, s32[1]{0:T(128)} %bitcast.1.own, bf16[8192,1024]{1,0:T(8,128)(2,1)} %bitcast.6, f32[1024,768]{1,0:T(8,128)S(1)} %score_pass.1.la_ref, f32[2,768]{1,0:T(2,128)S(1)} %pad_maximum_fusion.1.lse_ref, bf16[96,1024]{1,0:T(8,128)(2,1)} %collective-permute-done.13.refs_0_, ...), custom_call_target="tpu_custom_call" | custom-call | tf_op jit(solution)/shard_map/last_pass/pallas_call | solution.py:288
  (50 shorter events, 0.3 us)
Async XLA Ops:
  0.0 16.4 %copy-start.4 = (bf16[192,1024]{1,0:T(8,128)(2,1)S(1)}, bf16[192,1024]{1,0:T(8,128)(2,1)}, u32[]{:S(2)}) copy-start(bf16[192,1024]{1,0:T(8,128)(2,1)} %s_hbm.1) | copy-start | bytes 1179652
  14.1 2.1 %collective-permute-start = (f32[96,1280]{1,0:T(8,128)S(1)}, f32[96,1280]{1,0:T(8,128)S(1)}, u32[]{:S(2)}, u32[]{:S(2)}) collective-permute-start(f32[96,1280]{1,0:T(8,128)S(1)} %get-tuple-element.8), channel_id=1, source_target_pairs={{0,8},{8,0},{1,9},{9,1},{2,10},{10,2},{3,11},{11,3},{4,12},{12,4},... | collective-permute-start | bytes 1474568 | tf_op jit(solution)/shard_map/ppermute | solution.py:307
  16.6 8.1 %collective-permute-start.1 = (bf16[96,1024]{1,0:T(8,128)(2,1)S(1)}, bf16[96,1024]{1,0:T(8,128)(2,1)S(1)}, u32[]{:S(2)}, u32[]{:S(2)}) collective-permute-start(bf16[96,1024]{1,0:T(8,128)(2,1)S(1)} %subtract_convert_fusion), channel_id=1, source_target_pairs={{0,16},{1,17},{2,18},{3,19},{4,20},{5,21},{6,22},{7,23},{8,24},{9,... | collective-permute-start | bytes 589832 | tf_op jit(solution)/shard_map/ppermute | solution.py:319
  24.6 36.9 %copy-start.2 = (bf16[96,1024]{1,0:T(8,128)(2,1)}, bf16[96,1024]{1,0:T(8,128)(2,1)S(1)}, u32[]{:S(2)}) copy-start(bf16[96,1024]{1,0:T(8,128)(2,1)S(1)} %collective-permute-done.1.refs_0_.a_hbm.refs_8_) | copy-start | bytes 589828
  24.6 10.7 %collective-permute-start.2 = (bf16[96,1024]{1,0:T(8,128)(2,1)S(1)}, bf16[96,1024]{1,0:T(8,128)(2,1)S(1)}, u32[]{:S(2)}, u32[]{:S(2)}) collective-permute-start(bf16[96,1024]{1,0:T(8,128)(2,1)S(1)} %collective-permute-done.1.refs_0_.a_hbm.refs_8_), channel_id=1, source_target_pairs={{0,8},{8,0},{1,9},{9,1},{2,10},{10,2},{3,11},{11,3},{4,12},{12,4},... | collective-permute-start | bytes 589832 | tf_op jit(solution)/shard_map/ppermute | solution.py:307
  24.6 5.8 %copy-start = (bf16[1,8192,1024]{2,1,0:T(8,128)(2,1)S(1)}, bf16[1,8192,1024]{2,1,0:T(8,128)(2,1)}, u32[]{:S(2)}) copy-start(bf16[1,8192,1024]{2,1,0:T(8,128)(2,1)} %param.3) | copy-start | bytes 50331652
  30.5 5.8 %copy-start.1 = (bf16[1,8192,1024]{2,1,0:T(8,128)(2,1)S(1)}, bf16[1,8192,1024]{2,1,0:T(8,128)(2,1)}, u32[]{:S(2)}) copy-start(bf16[1,8192,1024]{2,1,0:T(8,128)(2,1)} %param.3) | copy-start | bytes 50331652
  30.5 20.3 %collective-permute-start.7 = (bf16[96,1024]{1,0:T(8,128)(2,1)S(1)}, bf16[96,1024]{1,0:T(8,128)(2,1)S(1)}, u32[]{:S(2)}, u32[]{:S(2)}) collective-permute-start(bf16[96,1024]{1,0:T(8,128)(2,1)S(1)} %subtract_convert_fusion), channel_id=1, source_target_pairs={{0,22},{1,23},{2,20},{3,21},{4,18},{5,19},{6,16},{7,17},{8,30},{9,... | collective-permute-start | bytes 589832 | tf_op jit(solution)/shard_map/ppermute | solution.py:319
  36.2 8.7 %copy-start.3 = (bf16[96,1024]{1,0:T(8,128)(2,1)}, bf16[96,1024]{1,0:T(8,128)(2,1)S(1)}, u32[]{:S(2)}) copy-start(bf16[96,1024]{1,0:T(8,128)(2,1)S(1)} %collective-permute-done.2.refs_1_.b_hbm.refs_9_) | copy-start | bytes 589828
  45.0 7.4 %collective-permute-start.9 = (f32[1,192]{1,0:T(1,128)S(1)}, f32[1,192]{1,0:T(1,128)S(1)}, u32[]{:S(2)}, u32[]{:S(2)}) collective-permute-start(f32[1,192]{1,0:T(1,128)S(1)} %stats_pass.1), channel_id=1, source_target_pairs={{0,8},{8,0},{1,9},{9,1},{2,10},{10,2},{3,11},{11,3},{4,12},{12,4},... | collective-permute-start | bytes 2312 | tf_op jit(solution)/shard_map/ppermute | solution.py:307
  45.5 13.2 %collective-permute-start.5 = (bf16[96,1024]{1,0:T(8,128)(2,1)S(1)}, bf16[96,1024]{1,0:T(8,128)(2,1)S(1)}, u32[]{:S(2)}, u32[]{:S(2)}) collective-permute-start(bf16[96,1024]{1,0:T(8,128)(2,1)S(1)} %subtract_convert_fusion), channel_id=1, source_target_pairs={{0,20},{1,21},{2,22},{3,23},{4,16},{5,17},{6,18},{7,19},{8,28},{9,... | collective-permute-start | bytes 589832 | tf_op jit(solution)/shard_map/ppermute | solution.py:319
  49.2 11.0 %collective-permute-start.3 = (bf16[96,1024]{1,0:T(8,128)(2,1)S(1)}, bf16[96,1024]{1,0:T(8,128)(2,1)S(1)}, u32[]{:S(2)}, u32[]{:S(2)}) collective-permute-start(bf16[96,1024]{1,0:T(8,128)(2,1)S(1)} %subtract_convert_fusion), channel_id=1, source_target_pairs={{0,18},{1,19},{2,16},{3,17},{4,22},{5,23},{6,20},{7,21},{8,26},{9,... | collective-permute-start | bytes 589832 | tf_op jit(solution)/shard_map/ppermute | solution.py:319
  50.8 11.7 %copy-start.5 = (bf16[96,1024]{1,0:T(8,128)(2,1)}, bf16[96,1024]{1,0:T(8,128)(2,1)S(1)}, u32[]{:S(2)}) copy-start(bf16[96,1024]{1,0:T(8,128)(2,1)S(1)} %collective-permute-done.7.refs_6_.refs_14_) | copy-start | bytes 589828
  50.8 9.5 %collective-permute-start.19 = (bf16[96,1024]{1,0:T(8,128)(2,1)S(1)}, bf16[96,1024]{1,0:T(8,128)(2,1)}, u32[]{:S(2)}, u32[]{:S(2)}) collective-permute-start(bf16[96,1024]{1,0:T(8,128)(2,1)S(1)} %collective-permute-done.7.refs_6_.refs_14_), channel_id=1, source_target_pairs={{0,1},{1,0},{2,3},{3,2},{4,5},{5,4},{6,7},{7,6},{8,9},{9,8},{10,11... | collective-permute-start | bytes 589832 | tf_op jit(solution)/shard_map/ppermute | solution.py:307
  52.3 9.2 %collective-permute-start.8 = (bf16[96,1024]{1,0:T(8,128)(2,1)S(1)}, bf16[96,1024]{1,0:T(8,128)(2,1)S(1)}, u32[]{:S(2)}, u32[]{:S(2)}) collective-permute-start(bf16[96,1024]{1,0:T(8,128)(2,1)S(1)} %collective-permute-done.7.refs_6_.refs_14_), channel_id=1, source_target_pairs={{0,8},{8,0},{1,9},{9,1},{2,10},{10,2},{3,11},{11,3},{4,12},{12,4},... | collective-permute-start | bytes 589832 | tf_op jit(solution)/shard_map/ppermute | solution.py:307
  52.4 4.9 %collective-permute-start.10 = (f32[1,192]{1,0:T(1,128)S(1)}, f32[1,192]{1,0:T(1,128)S(1)}, u32[]{:S(2)}, u32[]{:S(2)}) collective-permute-start(f32[1,192]{1,0:T(1,128)S(1)} %compare_select_fusion), channel_id=1, source_target_pairs={{0,1},{1,0},{2,3},{3,2},{4,5},{5,4},{6,7},{7,6},{8,9},{9,8},{10,11... | collective-permute-start | bytes 2312 | tf_op jit(solution)/shard_map/ppermute | solution.py:307
  57.2 5.2 %collective-permute-start.11 = (f32[2,192]{1,0:T(2,128)S(1)}, f32[2,192]{1,0:T(2,128)S(1)}, u32[]{:S(2)}, u32[]{:S(2)}) collective-permute-start(f32[2,192]{1,0:T(2,128)S(1)} %pad_maximum_fusion.3), channel_id=1, source_target_pairs={{0,2},{1,3},{2,0},{3,1},{4,6},{5,7},{6,4},{7,5},{8,10},{9,11},{10,... | collective-permute-start | bytes 4616 | tf_op jit(solution)/shard_map/ppermute | solution.py:307
  58.7 15.4 %copy-start.6 = (bf16[96,1024]{1,0:T(8,128)(2,1)}, bf16[96,1024]{1,0:T(8,128)(2,1)S(1)}, u32[]{:S(2)}) copy-start(bf16[96,1024]{1,0:T(8,128)(2,1)S(1)} %collective-permute-done.5.refs_4_.refs_12_) | copy-start | bytes 589828
  58.7 7.8 %collective-permute-start.17 = (bf16[96,1024]{1,0:T(8,128)(2,1)S(1)}, bf16[96,1024]{1,0:T(8,128)(2,1)}, u32[]{:S(2)}, u32[]{:S(2)}) collective-permute-start(bf16[96,1024]{1,0:T(8,128)(2,1)S(1)} %collective-permute-done.5.refs_4_.refs_12_), channel_id=1, source_target_pairs={{0,1},{1,0},{2,3},{3,2},{4,5},{5,4},{6,7},{7,6},{8,9},{9,8},{10,11... | collective-permute-start | bytes 589832 | tf_op jit(solution)/shard_map/ppermute | solution.py:307
  60.3 13.3 %copy-start.7 = (bf16[96,1024]{1,0:T(8,128)(2,1)}, bf16[96,1024]{1,0:T(8,128)(2,1)S(1)}, u32[]{:S(2)}) copy-start(bf16[96,1024]{1,0:T(8,128)(2,1)S(1)} %collective-permute-done.3.refs_2_.refs_10_) | copy-start | bytes 589828
  60.3 6.3 %collective-permute-start.6 = (bf16[96,1024]{1,0:T(8,128)(2,1)S(1)}, bf16[96,1024]{1,0:T(8,128)(2,1)S(1)}, u32[]{:S(2)}, u32[]{:S(2)}) collective-permute-start(bf16[96,1024]{1,0:T(8,128)(2,1)S(1)} %collective-permute-done.5.refs_4_.refs_12_), channel_id=1, source_target_pairs={{0,8},{8,0},{1,9},{9,1},{2,10},{10,2},{3,11},{11,3},{4,12},{12,4},... | collective-permute-start | bytes 589832 | tf_op jit(solution)/shard_map/ppermute | solution.py:307
  60.3 10.5 %collective-permute-start.15 = (bf16[96,1024]{1,0:T(8,128)(2,1)S(1)}, bf16[96,1024]{1,0:T(8,128)(2,1)}, u32[]{:S(2)}, u32[]{:S(2)}) collective-permute-start(bf16[96,1024]{1,0:T(8,128)(2,1)S(1)} %collective-permute-done.3.refs_2_.refs_10_), channel_id=1, source_target_pairs={{0,1},{1,0},{2,3},{3,2},{4,5},{5,4},{6,7},{7,6},{8,9},{9,8},{10,11... | collective-permute-start | bytes 589832 | tf_op jit(solution)/shard_map/ppermute | solution.py:307
  61.5 12.0 %copy-start.8 = (bf16[96,1024]{1,0:T(8,128)(2,1)}, bf16[96,1024]{1,0:T(8,128)(2,1)S(1)}, u32[]{:S(2)}) copy-start(bf16[96,1024]{1,0:T(8,128)(2,1)S(1)} %collective-permute-done.8.refs_7_.refs_15_) | copy-start | bytes 589828
  61.5 11.9 %collective-permute-start.13 = (bf16[96,1024]{1,0:T(8,128)(2,1)S(1)}, bf16[96,1024]{1,0:T(8,128)(2,1)}, u32[]{:S(2)}, u32[]{:S(2)}) collective-permute-start(bf16[96,1024]{1,0:T(8,128)(2,1)S(1)} %collective-permute-done.1.refs_0_.a_hbm.refs_8_), channel_id=1, source_target_pairs={{0,1},{1,0},{2,3},{3,2},{4,5},{5,4},{6,7},{7,6},{8,9},{9,8},{10,11... | collective-permute-start | bytes 589832 | tf_op jit(solution)/shard_map/ppermute | solution.py:307
  62.4 11.0 %collective-permute-start.4 = (bf16[96,1024]{1,0:T(8,128)(2,1)S(1)}, bf16[96,1024]{1,0:T(8,128)(2,1)S(1)}, u32[]{:S(2)}, u32[]{:S(2)}) collective-permute-start(bf16[96,1024]{1,0:T(8,128)(2,1)S(1)} %collective-permute-done.3.refs_2_.refs_10_), channel_id=1, source_target_pairs={{0,8},{8,0},{1,9},{9,1},{2,10},{10,2},{3,11},{11,3},{4,12},{12,4},... | collective-permute-start | bytes 589832 | tf_op jit(solution)/shard_map/ppermute | solution.py:307
  66.5 11.8 %collective-permute-start.20 = (bf16[96,1024]{1,0:T(8,128)(2,1)}, bf16[96,1024]{1,0:T(8,128)(2,1)}, u32[]{:S(2)}, u32[]{:S(2)}) collective-permute-start(bf16[96,1024]{1,0:T(8,128)(2,1)} %collective-permute-done.19.refs_6_), channel_id=1, source_target_pairs={{0,8},{8,0},{1,9},{9,1},{2,10},{10,2},{3,11},{11,3},{4,12},{12,4},... | collective-permute-start | bytes 589832 | tf_op jit(solution)/shard_map/ppermute | solution.py:307
  66.5 7.0 %copy-start.9 = (bf16[96,1024]{1,0:T(8,128)(2,1)}, bf16[96,1024]{1,0:T(8,128)(2,1)S(1)}, u32[]{:S(2)}) copy-start(bf16[96,1024]{1,0:T(8,128)(2,1)S(1)} %collective-permute-done.6.refs_5_.refs_13_) | copy-start | bytes 589828
  66.5 11.8 %collective-permute-start.18 = (bf16[96,1024]{1,0:T(8,128)(2,1)}, bf16[96,1024]{1,0:T(8,128)(2,1)}, u32[]{:S(2)}, u32[]{:S(2)}) collective-permute-start(bf16[96,1024]{1,0:T(8,128)(2,1)} %collective-permute-done.17.refs_4_), channel_id=1, source_target_pairs={{0,8},{8,0},{1,9},{9,1},{2,10},{10,2},{3,11},{11,3},{4,12},{12,4},... | collective-permute-start | bytes 589832 | tf_op jit(solution)/shard_map/ppermute | solution.py:307
  70.7 7.6 %collective-permute-start.16 = (bf16[96,1024]{1,0:T(8,128)(2,1)}, bf16[96,1024]{1,0:T(8,128)(2,1)}, u32[]{:S(2)}, u32[]{:S(2)}) collective-permute-start(bf16[96,1024]{1,0:T(8,128)(2,1)} %collective-permute-done.15.refs_2_), channel_id=1, source_target_pairs={{0,8},{8,0},{1,9},{9,1},{2,10},{10,2},{3,11},{11,3},{4,12},{12,4},... | collective-permute-start | bytes 589832 | tf_op jit(solution)/shard_map/ppermute | solution.py:307
  73.4 5.0 %collective-permute-start.14 = (bf16[96,1024]{1,0:T(8,128)(2,1)}, bf16[96,1024]{1,0:T(8,128)(2,1)S(1)}, u32[]{:S(2)}, u32[]{:S(2)}) collective-permute-start(bf16[96,1024]{1,0:T(8,128)(2,1)} %collective-permute-done.13.refs_0_), channel_id=1, source_target_pairs={{0,8},{8,0},{1,9},{9,1},{2,10},{10,2},{3,11},{11,3},{4,12},{12,4},... | collective-permute-start | bytes 589832 | tf_op jit(solution)/shard_map/ppermute | solution.py:307
  73.4 0.7 copy-start.10
  73.4 4.7 %collective-permute-start.12 = (f32[4,192]{1,0:T(4,128)S(1)}, f32[4,192]{1,0:T(4,128)S(1)}, u32[]{:S(2)}, u32[]{:S(2)}) collective-permute-start(f32[4,192]{1,0:T(4,128)S(1)} %pad_maximum_fusion.2), channel_id=1, source_target_pairs={{0,4},{1,5},{2,6},{3,7},{4,0},{5,1},{6,2},{7,3},{8,12},{9,13},{10,... | collective-permute-start | bytes 9224 | tf_op jit(solution)/shard_map/ppermute | solution.py:307
  (1 other events, 0.7 us)
